TPU v7x, 256 devices: a whole 4x4x8 slice. The times are simulated.
256 devices in a mesh: section: 4 (over x), owner: 64 (over z, y, core).
Axes of the slice: x: 4, y: 4, z: 8, core: 2. Of those that a mesh axis runs over, the one named last changes fastest.
Arguments:
- probe_values: bfloat16 [8, 524288, 128], P('section', 'owner'), may hold values from -6 to 6
- probe_keys: int32 [8, 524288], P('section', 'owner'), may hold values from 0 to 2047
- group_ids: int32 [8, 524288], P('section', 'owner'), may hold values from 0 to 1023
- block_dest: int32 [8, 4096, 1], P('section', 'owner'), may hold values from 0 to 63; in each aligned block of 64 rows (0 to 63, 64 to 127, ..., all dimensions but the last counted through in order) at most 2 rows name the same one
- filter_bits: int32 [4, 8, 32768], P('section', None, 'owner'), may hold values from 0 to 65535, as said below
- section_weights: bfloat16 [4, 128, 128], P('section'), may hold values from -0.5 to 0.5
- build_keys: int32 [262144], P('owner'), may hold values from 0 to 2047
- build_values: bfloat16 [262144, 128], P('owner'), may hold values from -6 to 6
Outputs:
- group_sums: float32 [1024, 128], P(('section', 'owner'))
Inputs may be any that keep to these rules, and one draw needn't show every extreme that they name: `block_dest`: in each micro-batch, no owner is named by more than 2 of the 64 blocks of one device, a bound that some block reaches. `filter_bits`: bit b of a word is the keep bit of row 16 w + b; the upper bits are 0.
All inputs are finite; a program needn't handle non-finite values.
Results may differ from a plain program's by a relative error of at most 0.012.
Values may be sent and summed in bfloat16 or wider, within the bound.
A program may use at most 128 MiB of HBM per device.

v0:
```python
import jax
import jax.numpy as jnp
from jax import lax
from jax.sharding import Mesh
from jax.sharding import PartitionSpec as P

CAP = 2
KEYS_OWN = 2048
GRP_DEV = 4
OWNER = ("owner_0", "owner_1", "owner_2")
SECTION_OWNER = ("section", "owner_0", "owner_1", "owner_2")


def in_order(pieces, dim):
    dims = list(pieces.shape[1:])
    dims[dim] *= pieces.shape[0]
    return jnp.moveaxis(pieces, 0, dim).reshape(dims)


def copy_for_each(x, axis):
    size = lax.axis_size(axis)
    return lax.all_to_all(jnp.broadcast_to(x[None], (size, *x.shape)), axis, 0, 0, tiled=True)


def collect(x, axis, dim):
    return in_order(copy_for_each(x, axis), dim)


def cut_along(x, dim, size):
    before, after = (x.shape[:dim], x.shape[dim + 1 :])
    return jnp.moveaxis(x.reshape(*before, size, -1, *after), dim, 0)


def summed_on_arrival(x, axis, dim):
    size = lax.axis_size(axis)
    pieces = lax.all_to_all(cut_along(x, dim, size), axis, 0, 0, tiled=True)
    return jnp.sum(pieces, axis=0)


def summed_rows(x, axes, dim):
    far, near = axes
    own = summed_on_arrival(cut_along(x, dim, lax.axis_size(far)), near, dim + 1)
    return jnp.sum(lax.all_to_all(own, far, 0, 0, tiled=True), axis=0)


def unpack_bits(bit_words):
    shifts = jnp.arange(16, dtype=jnp.int32)
    spread = jnp.right_shift(bit_words[..., None], shifts) & 1
    return spread.reshape(bit_words.shape[:-1] + (bit_words.shape[-1] * 16,)).astype(jnp.float32)


def apply_section(payload, kept_mask, weight):
    columns = payload.shape[-1]
    projected = jnp.dot(payload.reshape(-1, columns), weight, preferred_element_type=jnp.float32)
    projected = projected.reshape(payload.shape)
    updated = kept_mask[..., None] * (payload.astype(jnp.float32) + jax.nn.silu(projected))
    return updated.astype(jnp.bfloat16)


def pick_blocks(table_rows, picks):
    return jnp.take(table_rows, picks.reshape(-1), axis=0).reshape(
        picks.shape + table_rows.shape[1:]
    )


def local(
    probe_values,
    probe_keys,
    group_ids,
    block_dest,
    filter_bits,
    section_weights,
    build_keys,
    build_values,
):
    section_count = lax.axis_size("section")
    owner_count = lax.axis_size(OWNER)
    section_index = lax.axis_index("section")
    batches = probe_values.shape[0]
    block_count = block_dest.shape[1]
    columns = probe_values.shape[2]
    block_rows = probe_values.shape[1] // block_count
    groups_all = GRP_DEV * section_count * owner_count
    payload = probe_values
    all_weights, all_bits = (
        collect(section_weights, "section", 0),
        collect(filter_bits, "section", 0),
    )
    for step_number in range(section_count):
        source_section = (section_index + step_number) % section_count
        weight = lax.dynamic_index_in_dim(all_weights, source_section, 0, keepdims=False)
        section_bits = lax.dynamic_index_in_dim(all_bits, source_section, 0, keepdims=False)
        bit_words = lax.dynamic_slice_in_dim(section_bits, section_index * batches, batches, 0)
        payload = apply_section(payload, unpack_bits(bit_words), weight)
    row_keys, row_groups, row_dest = (probe_keys, group_ids, block_dest)
    destination = row_dest[:, :, 0]
    owner_ids = jnp.arange(owner_count, dtype=jnp.int32)
    chosen = (destination[:, :, None] == owner_ids).astype(jnp.int32)
    earlier = jnp.cumsum(chosen, axis=1) - chosen
    slot_index = jnp.sum(earlier * chosen, axis=2)
    capacity = CAP
    slot_ids = jnp.arange(capacity, dtype=jnp.int32)
    matching = chosen[:, :, :, None] * (slot_index[:, :, None, None] == slot_ids).astype(jnp.int32)
    block_ids = jnp.arange(block_count, dtype=jnp.int32)
    source_block = (
        jnp.sum(matching * (block_ids[None, :, None, None] - block_count), axis=1) + block_count
    )
    blocks = payload.reshape(batches, block_count, block_rows, columns)
    blocks = jnp.concatenate(
        [blocks, jnp.zeros((batches, 1, block_rows, columns), jnp.bfloat16)], axis=1
    )
    key_blocks = row_keys.reshape(batches, block_count, block_rows)
    key_blocks = jnp.concatenate(
        [key_blocks, jnp.zeros((batches, 1, block_rows), jnp.int32)], axis=1
    )
    group_blocks = row_groups.reshape(batches, block_count, block_rows)
    group_blocks = jnp.concatenate(
        [group_blocks, jnp.zeros((batches, 1, block_rows), jnp.int32)], axis=1
    )
    send_values = jax.vmap(pick_blocks)(blocks, source_block)
    send_keys = jax.vmap(pick_blocks)(key_blocks, source_block)
    send_groups = jax.vmap(pick_blocks)(group_blocks, source_block)
    key_table = jax.ops.segment_sum(
        build_values.astype(jnp.float32), build_keys, num_segments=KEYS_OWN
    )
    group_range = jnp.arange(groups_all, dtype=jnp.int32)
    group_span = min(owner_count, 8)

    def add_block(running, pieces):
        part_values, part_keys, part_groups = pieces
        matched = jnp.take(key_table, part_keys, axis=0)
        joined = (part_values.astype(jnp.float32) * matched).astype(jnp.bfloat16)
        onehot = (part_groups[:, None] == group_range).astype(jnp.bfloat16)
        running = running + lax.dot_general(
            onehot, joined, (((0,), (0,)), ((), ())), preferred_element_type=jnp.float32
        )
        return (running, None)

    def join_item(received_item):
        item_values, item_keys, item_groups = received_item
        sources = item_values.shape[0]
        steps_count = sources // group_span
        rows_values = item_values.reshape(steps_count, -1, columns)
        rows_keys = item_keys.reshape(steps_count, -1)
        rows_groups = item_groups.reshape(steps_count, -1)
        running, unused = lax.scan(
            add_block,
            jnp.zeros((groups_all, columns), jnp.float32),
            (rows_values, rows_keys, rows_groups),
        )
        return running

    partials = lax.map(
        join_item,
        (
            lax.all_to_all(send_values, OWNER, split_axis=1, concat_axis=1, tiled=True),
            lax.all_to_all(send_keys, OWNER, split_axis=1, concat_axis=1, tiled=True),
            lax.all_to_all(send_groups, OWNER, split_axis=1, concat_axis=1, tiled=True),
        ),
    )
    partial_sum = jnp.sum(partials, axis=0)
    return summed_rows(partial_sum, (("section", "owner_0"), ("owner_1", "owner_2")), 0)


def solution(mesh):
    torus = Mesh(
        mesh.devices.reshape(mesh.shape["section"], 8, 4, 2),
        ("section", "owner_0", "owner_1", "owner_2"),
    )
    return jax.shard_map(
        local,
        mesh=torus,
        in_specs=(
            P("section", OWNER, None),
            P("section", OWNER),
            P("section", OWNER),
            P("section", OWNER, None),
            P("section", None, OWNER),
            P("section", None, None),
            P(OWNER),
            P(OWNER, None),
        ),
        out_specs=P(SECTION_OWNER, None),
        check_vma=False,
    )
```

profile of v0, /device:TPU:1, one launch (start us, length us, event | category | flops | bytes accessed | tf_op | source)
XLA Modules:
  0.0 515.5 jit_solution(106723879779317992)
XLA Ops:
  25.5 14.3 %all-to-all-start.3 = ((s32[2,64,2,128]{3,2,0,1:T(2,128)}), s32[2,64,2,128]{3,2,0,1:T(2,128)S(1)}, u32[]{:S(2)}, u32[]{:S(2)}) async-start(s32[2,64,2,128]{3,2,0,1:T(2,128)} %copy.48), calls=%async_computation.3 | async-start | bytes 262144 | tf_op jit(solution)/shard_map/all_to_all | solution.py:157
  39.8 6.7 %convolution_bitcast_fusion = f32[16384,128]{0,1:T(8,128)} fusion(bf16[16384,128]{1,0:T(8,128)(2,1)} %bitcast.99, bf16[4,1,128,128]{3,2,1,0:T(8,128)(2,1)S(1)} %all-to-all-done.1, s32[]{:T(128)S(6)} %select_n.114), kind=kOutput, calls=%fused_computation.29 | convolution fusion | flops 536870912 | bytes 12615684 | tf_op jit(solution)/shard_map/dot_general | solution.py:54
  46.5 9.0 %copy.55 = f32[16384,128]{1,0:T(8,128)} copy(f32[16384,128]{0,1:T(8,128)} %convolution_bitcast_fusion) | data formatting | bytes 16777216 | tf_op jit(solution)/shard_map/reshape | solution.py:55
  55.5 16.7 %multiply_convert_fusion.2 = bf16[2,8192,128]{2,1,0:T(8,128)(2,1)S(1)} fusion(f32[2,8192]{1,0:T(2,128)S(1)} %get-tuple-element.187, f32[2,8192,128]{2,1,0:T(8,128)} %bitcast.97, bf16[2,8192,128]{2,1,0:T(8,128)(2,1)} %param.14, f32[2,8192]{1,0:T(2,128)S(1)} %get-tuple-element.188, bf16[4,1,128,128]{3,2,1,0:T(8,128)(2,1)S(1)} %all-to-all-done.1, ...), kind=kOutput, calls=%fused_computation.32 | convolution fusion | flops 587202560 | bytes 29589508 | tf_op jit(solution)/shard_map/dot_general | solution.py:54
  83.2 12.3 %gather_fusion.1 = bf16[256,128,128]{2,1,0:T(8,128)(2,1)} fusion(bf16[2,65,128,128]{3,2,1,0:T(8,128)(2,1)} %concatenate.9, s32[256]{0:T(256)S(1)} %get-tuple-element.194), kind=kCustom, calls=%fused_computation.3 | custom fusion | bytes 16779264 | tf_op jit(solution)/shard_map/vmap(jit(_take))/gather | solution.py:61
  95.4 10.3 %all-to-all-start.4 = ((s32[2,64,2,128]{3,2,0,1:T(2,128)}), s32[2,64,2,128]{3,2,0,1:T(2,128)S(1)}, u32[]{:S(2)}, u32[]{:S(2)}) async-start(s32[2,64,2,128]{3,2,0,1:T(2,128)} %copy.49), calls=%async_computation.4 | async-start | bytes 262144 | tf_op jit(solution)/shard_map/all_to_all | solution.py:158
  105.8 7.4 %broadcast_select_fusion = bf16[2,64,2,128,128]{4,3,2,1,0:T(8,128)(2,1)} fusion(bf16[2,64,2,128,128]{4,3,2,1,0:T(8,128)(2,1)} %bitcast.94, pred[2,64,2]{2,1,0:T(8,128)(4,1)S(1)} %copy.41), kind=kLoop, calls=%fused_computation.34 | loop fusion | flops 4194304 | bytes 16777472 | tf_op jit(solution)/shard_map/vmap(jit(_take))/select_n | solution.py:61
  113.2 10.3 %copy.46 = bf16[2,64,2,128,128]{4,3,2,0,1:T(8,128)(2,1)} copy(bf16[2,64,2,128,128]{4,3,2,1,0:T(8,128)(2,1)} %broadcast_select_fusion) | data formatting | bytes 16777216 | tf_op jit(solution)/shard_map/vmap(jit(_take))/select_n | solution.py:61
  123.5 10.8 %all-to-all-start.2 = ((bf16[2,64,2,128,128]{4,3,2,0,1:T(8,128)(2,1)}), bf16[2,64,2,128,128]{4,3,2,0,1:T(8,128)(2,1)}, u32[]{:S(2)}, u32[]{:S(2)}) async-start(bf16[2,64,2,128,128]{4,3,2,0,1:T(8,128)(2,1)} %copy.46), calls=%async_computation.2 | async-start | bytes 16777216 | tf_op jit(solution)/shard_map/all_to_all | solution.py:156
  134.4 22.8 %scatter_custom_fusion = f32[2048,128]{1,0:T(8,128)S(1)} fusion(s32[4096]{0:T(1024)} %param.20, bf16[4096,128]{1,0:T(8,128)(2,1)S(1)} %copy-done, f32[]{:T(128)} %constant.222.clone.1), kind=kCustom, calls=%fused_computation.35 | custom fusion | flops 1048576 | bytes 2097664 | tf_op jit(solution)/shard_map/scatter-add | solution.py:123
  157.2 159.5 %all-to-all-done.2 = bf16[2,64,2,128,128]{4,3,2,0,1:T(8,128)(2,1)} async-done(((bf16[2,64,2,128,128]{4,3,2,0,1:T(8,128)(2,1)}), bf16[2,64,2,128,128]{4,3,2,0,1:T(8,128)(2,1)}, u32[]{:S(2)}, u32[]{:S(2)}) %all-to-all-start.2) | async-done | bytes 8388640 | tf_op jit(solution)/shard_map/all_to_all | solution.py:156
  316.7 166.8 %while.24 = (s32[]{:T(128)}, f32[2,1024,128]{2,1,0:T(8,128)}, bf16[2,64,2,128,128]{4,3,2,0,1:T(8,128)(2,1)}, s32[2,64,2,128]{3,2,0,1:T(2,128)S(1)}, s32[2,64,2,1...) while((s32[]{:T(128)}, f32[2,1024,128]{2,1,0:T(8,128)}, ...), condition=%wide.region_7.9_spmd.clone, body=%wide.region_4.8_spmd.clone.sunk | while | flops 540299264 | bytes 14775596 | solution.py:153
  321.6 77.6 %while.25 = (s32[]{:T(128)}, f32[1024,128]{1,0:T(8,128)S(1)}, s32[8,2048]{1,0:T(8,128)S(1)}, s32[1024]{0:T(1024)S(1)}, bf16[8,2048,128]{2,1,0:T(8,128)(2,1)}, /*...) while((s32[]{:T(128)}, f32[1024,128]{1,0:T(8,128)S(1)}, ...), condition=%wide.region_6.7_spmd.clone, body=%wide.region_5.6_spmd.clone.sunk | while | flops 540299264 | bytes 4809327 | solution.py:146
  321.6 5.5 %gather_fusion = f32[2048,128]{1,0:T(8,128)S(1)} fusion(f32[2048,128]{1,0:T(8,128)S(1)} %get-tuple-element.324, s32[2048]{0:T(1024)S(1)} %broadcast_clamp_fusion.2), kind=kCustom, calls=%fused_computation.1.clone.clone.1 | custom fusion | bytes 2105344 | tf_op jit(solution)/shard_map/while/body/eval_jaxpr/while/body/eval_jaxpr/jit(_take)/gather | solution.py:131
  331.3 5.5 %gather_fusion = f32[2048,128]{1,0:T(8,128)S(1)} fusion(f32[2048,128]{1,0:T(8,128)S(1)} %get-tuple-element.324, s32[2048]{0:T(1024)S(1)} %broadcast_clamp_fusion.2), kind=kCustom, calls=%fused_computation.1.clone.clone.1 | custom fusion | bytes 2105344 | tf_op jit(solution)/shard_map/while/body/eval_jaxpr/while/body/eval_jaxpr/jit(_take)/gather | solution.py:131
  341.0 5.5 %gather_fusion = f32[2048,128]{1,0:T(8,128)S(1)} fusion(f32[2048,128]{1,0:T(8,128)S(1)} %get-tuple-element.324, s32[2048]{0:T(1024)S(1)} %broadcast_clamp_fusion.2), kind=kCustom, calls=%fused_computation.1.clone.clone.1 | custom fusion | bytes 2105344 | tf_op jit(solution)/shard_map/while/body/eval_jaxpr/while/body/eval_jaxpr/jit(_take)/gather | solution.py:131
  350.8 5.5 %gather_fusion = f32[2048,128]{1,0:T(8,128)S(1)} fusion(f32[2048,128]{1,0:T(8,128)S(1)} %get-tuple-element.324, s32[2048]{0:T(1024)S(1)} %broadcast_clamp_fusion.2), kind=kCustom, calls=%fused_computation.1.clone.clone.1 | custom fusion | bytes 2105344 | tf_op jit(solution)/shard_map/while/body/eval_jaxpr/while/body/eval_jaxpr/jit(_take)/gather | solution.py:131
  360.5 5.5 %gather_fusion = f32[2048,128]{1,0:T(8,128)S(1)} fusion(f32[2048,128]{1,0:T(8,128)S(1)} %get-tuple-element.324, s32[2048]{0:T(1024)S(1)} %broadcast_clamp_fusion.2), kind=kCustom, calls=%fused_computation.1.clone.clone.1 | custom fusion | bytes 2105344 | tf_op jit(solution)/shard_map/while/body/eval_jaxpr/while/body/eval_jaxpr/jit(_take)/gather | solution.py:131
  370.2 5.5 %gather_fusion = f32[2048,128]{1,0:T(8,128)S(1)} fusion(f32[2048,128]{1,0:T(8,128)S(1)} %get-tuple-element.324, s32[2048]{0:T(1024)S(1)} %broadcast_clamp_fusion.2), kind=kCustom, calls=%fused_computation.1.clone.clone.1 | custom fusion | bytes 2105344 | tf_op jit(solution)/shard_map/while/body/eval_jaxpr/while/body/eval_jaxpr/jit(_take)/gather | solution.py:131
  379.9 5.5 %gather_fusion = f32[2048,128]{1,0:T(8,128)S(1)} fusion(f32[2048,128]{1,0:T(8,128)S(1)} %get-tuple-element.324, s32[2048]{0:T(1024)S(1)} %broadcast_clamp_fusion.2), kind=kCustom, calls=%fused_computation.1.clone.clone.1 | custom fusion | bytes 2105344 | tf_op jit(solution)/shard_map/while/body/eval_jaxpr/while/body/eval_jaxpr/jit(_take)/gather | solution.py:131
  389.6 5.5 %gather_fusion = f32[2048,128]{1,0:T(8,128)S(1)} fusion(f32[2048,128]{1,0:T(8,128)S(1)} %get-tuple-element.324, s32[2048]{0:T(1024)S(1)} %broadcast_clamp_fusion.2), kind=kCustom, calls=%fused_computation.1.clone.clone.1 | custom fusion | bytes 2105344 | tf_op jit(solution)/shard_map/while/body/eval_jaxpr/while/body/eval_jaxpr/jit(_take)/gather | solution.py:131
  405.0 77.6 %while.25 = (s32[]{:T(128)}, f32[1024,128]{1,0:T(8,128)S(1)}, s32[8,2048]{1,0:T(8,128)S(1)}, s32[1024]{0:T(1024)S(1)}, bf16[8,2048,128]{2,1,0:T(8,128)(2,1)}, /*...) while((s32[]{:T(128)}, f32[1024,128]{1,0:T(8,128)S(1)}, ...), condition=%wide.region_6.7_spmd.clone, body=%wide.region_5.6_spmd.clone.sunk | while | flops 540299264 | bytes 4809327 | solution.py:146
  405.0 5.5 %gather_fusion = f32[2048,128]{1,0:T(8,128)S(1)} fusion(f32[2048,128]{1,0:T(8,128)S(1)} %get-tuple-element.324, s32[2048]{0:T(1024)S(1)} %broadcast_clamp_fusion.2), kind=kCustom, calls=%fused_computation.1.clone.clone.1 | custom fusion | bytes 2105344 | tf_op jit(solution)/shard_map/while/body/eval_jaxpr/while/body/eval_jaxpr/jit(_take)/gather | solution.py:131
  414.7 5.5 %gather_fusion = f32[2048,128]{1,0:T(8,128)S(1)} fusion(f32[2048,128]{1,0:T(8,128)S(1)} %get-tuple-element.324, s32[2048]{0:T(1024)S(1)} %broadcast_clamp_fusion.2), kind=kCustom, calls=%fused_computation.1.clone.clone.1 | custom fusion | bytes 2105344 | tf_op jit(solution)/shard_map/while/body/eval_jaxpr/while/body/eval_jaxpr/jit(_take)/gather | solution.py:131
  424.4 5.5 %gather_fusion = f32[2048,128]{1,0:T(8,128)S(1)} fusion(f32[2048,128]{1,0:T(8,128)S(1)} %get-tuple-element.324, s32[2048]{0:T(1024)S(1)} %broadcast_clamp_fusion.2), kind=kCustom, calls=%fused_computation.1.clone.clone.1 | custom fusion | bytes 2105344 | tf_op jit(solution)/shard_map/while/body/eval_jaxpr/while/body/eval_jaxpr/jit(_take)/gather | solution.py:131
  434.1 5.5 %gather_fusion = f32[2048,128]{1,0:T(8,128)S(1)} fusion(f32[2048,128]{1,0:T(8,128)S(1)} %get-tuple-element.324, s32[2048]{0:T(1024)S(1)} %broadcast_clamp_fusion.2), kind=kCustom, calls=%fused_computation.1.clone.clone.1 | custom fusion | bytes 2105344 | tf_op jit(solution)/shard_map/while/body/eval_jaxpr/while/body/eval_jaxpr/jit(_take)/gather | solution.py:131
  443.8 5.5 %gather_fusion = f32[2048,128]{1,0:T(8,128)S(1)} fusion(f32[2048,128]{1,0:T(8,128)S(1)} %get-tuple-element.324, s32[2048]{0:T(1024)S(1)} %broadcast_clamp_fusion.2), kind=kCustom, calls=%fused_computation.1.clone.clone.1 | custom fusion | bytes 2105344 | tf_op jit(solution)/shard_map/while/body/eval_jaxpr/while/body/eval_jaxpr/jit(_take)/gather | solution.py:131
  453.6 5.5 %gather_fusion = f32[2048,128]{1,0:T(8,128)S(1)} fusion(f32[2048,128]{1,0:T(8,128)S(1)} %get-tuple-element.324, s32[2048]{0:T(1024)S(1)} %broadcast_clamp_fusion.2), kind=kCustom, calls=%fused_computation.1.clone.clone.1 | custom fusion | bytes 2105344 | tf_op jit(solution)/shard_map/while/body/eval_jaxpr/while/body/eval_jaxpr/jit(_take)/gather | solution.py:131
  463.3 5.5 %gather_fusion = f32[2048,128]{1,0:T(8,128)S(1)} fusion(f32[2048,128]{1,0:T(8,128)S(1)} %get-tuple-element.324, s32[2048]{0:T(1024)S(1)} %broadcast_clamp_fusion.2), kind=kCustom, calls=%fused_computation.1.clone.clone.1 | custom fusion | bytes 2105344 | tf_op jit(solution)/shard_map/while/body/eval_jaxpr/while/body/eval_jaxpr/jit(_take)/gather | solution.py:131
  473.0 5.5 %gather_fusion = f32[2048,128]{1,0:T(8,128)S(1)} fusion(f32[2048,128]{1,0:T(8,128)S(1)} %get-tuple-element.324, s32[2048]{0:T(1024)S(1)} %broadcast_clamp_fusion.2), kind=kCustom, calls=%fused_computation.1.clone.clone.1 | custom fusion | bytes 2105344 | tf_op jit(solution)/shard_map/while/body/eval_jaxpr/while/body/eval_jaxpr/jit(_take)/gather | solution.py:131
  484.9 17.1 %all_to_all.35 = f32[8,32,4,128]{3,2,1,0:T(4,128)S(1)} all-to-all(f32[8,32,4,128]{3,2,1,0:T(4,128)S(1)} %copy.53), channel_id=1, replica_groups=mesh['section'=4,'owner_0'=8,'owner_1'=4,'owner_2'=2] {'owner_1','owner_2'}, dimensions={0} | all-to-all | bytes 1048576 | tf_op jit(solution)/shard_map/all_to_all | solution.py:36
  502.1 12.9 %all_to_all.36 = f32[32,4,128]{2,1,0:T(4,128)S(1)} all-to-all(f32[32,4,128]{2,1,0:T(4,128)S(1)} %reduce_sum.48), channel_id=1, replica_groups=mesh['section'=4,'owner_0'=8,'owner_1'=4,'owner_2'=2] {'section','owner_0'}, dimensions={0} | all-to-all | bytes 131072 | tf_op jit(solution)/shard_map/all_to_all | solution.py:43
  (147 shorter events, 116.7 us)
Async XLA Ops:
  1.3 13.7 %all-to-all-start = ((s32[4,1,8,512]{3,2,1,0:T(8,128)}), s32[4,1,8,512]{3,2,1,0:T(8,128)S(1)}, u32[]{:S(2)}, u32[]{:S(2)}) async-start(s32[4,1,8,512]{3,2,1,0:T(8,128)} %broadcast_in_dim.51), calls=%async_computation | async-start | bytes 131072 | tf_op jit(solution)/shard_map/all_to_all | solution.py:22
  16.5 9.1 %all-to-all-start.1 = ((bf16[4,1,128,128]{3,2,1,0:T(8,128)(2,1)}), bf16[4,1,128,128]{3,2,1,0:T(8,128)(2,1)S(1)}, u32[]{:S(2)}, u32[]{:S(2)}) async-start(bf16[4,1,128,128]{3,2,1,0:T(8,128)(2,1)} %broadcast_in_dim.83), calls=%async_computation.1 | async-start | bytes 262144 | tf_op jit(solution)/shard_map/all_to_all | solution.py:22
  25.5 69.9 %all-to-all-start.3 = ((s32[2,64,2,128]{3,2,0,1:T(2,128)}), s32[2,64,2,128]{3,2,0,1:T(2,128)S(1)}, u32[]{:S(2)}, u32[]{:S(2)}) async-start(s32[2,64,2,128]{3,2,0,1:T(2,128)} %copy.48), calls=%async_computation.3 | async-start | bytes 262144 | tf_op jit(solution)/shard_map/all_to_all | solution.py:157
  95.4 28.1 %all-to-all-start.4 = ((s32[2,64,2,128]{3,2,0,1:T(2,128)}), s32[2,64,2,128]{3,2,0,1:T(2,128)S(1)}, u32[]{:S(2)}, u32[]{:S(2)}) async-start(s32[2,64,2,128]{3,2,0,1:T(2,128)} %copy.49), calls=%async_computation.4 | async-start | bytes 262144 | tf_op jit(solution)/shard_map/all_to_all | solution.py:158
  123.5 10.9 %copy-start = (bf16[4096,128]{1,0:T(8,128)(2,1)S(1)}, bf16[4096,128]{1,0:T(8,128)(2,1)}, u32[]{:S(2)}) copy-start(bf16[4096,128]{1,0:T(8,128)(2,1)} %param.21) | copy-start | bytes 3145732
  123.5 193.1 %all-to-all-start.2 = ((bf16[2,64,2,128,128]{4,3,2,0,1:T(8,128)(2,1)}), bf16[2,64,2,128,128]{4,3,2,0,1:T(8,128)(2,1)}, u32[]{:S(2)}, u32[]{:S(2)}) async-start(bf16[2,64,2,128,128]{4,3,2,0,1:T(8,128)(2,1)} %copy.46), calls=%async_computation.2 | async-start | bytes 16777216 | tf_op jit(solution)/shard_map/all_to_all | solution.py:156
where the time goes:
time: 518 us; the launch traced here: 516 us
  waiting for transfers between devices  162 us (31%)
  local copies, waits for them, and re-layouts  145 us (28%)
  matrix products  97.6 us (19%)
  starting transfers between devices  44.5 us (9%)
  other arithmetic  34.9 us (7%)
  blocking collectives  29.9 us (6%)
    all_to_all x1, waiting for transfers between devices, local(): lax.all_to_all(send_values, OWNER, split_axis=1, concat_axis=1, tiled=True)  159 us
    gather x16, local copies, waits for them, and re-layouts, add_block(): matched = jnp.take(key_table, part_keys, axis=0)  87.4 us
    dot_general x16, matrix products, add_block(): lax.dot_general(onehot, joined, (((0,), (0,)), ((), ())), preferred_eleme...  66.1 us
    dot_general x4, matrix products, apply_section(): jnp.dot(payload.reshape(-1, columns), weight, preferred_element_type=jnp....  31.5 us
    scatter-add x1, other arithmetic, local(): jax.ops.segment_sum(build_values.astype(jnp.float32), build_keys, num_seg...  22.8 us
    all_to_all x1, blocking collectives, summed_on_arrival(): pieces = lax.all_to_all(cut_along(x, dim, size), axis, 0, 0, tiled=True)  17.1 us
    gather x3, local copies, waits for them, and re-layouts, pick_blocks(): jnp.take(table_rows, picks.reshape(-1), axis=0)  14.9 us
    all_to_all x1, starting transfers between devices, local(): lax.all_to_all(send_keys, OWNER, split_axis=1, concat_axis=1, tiled=True)  14.3 us
  transfers between devices with their start and end apart: 5, of which 2 were waited for; matrix products, arithmetic and copies ran while one was open for 21% of the time, Pallas kernels for 0%

commit v1 on v0

v1 whole, which is shorter than its diff:
```python
import functools

import jax
import jax.numpy as jnp
from jax import lax
from jax.experimental import pallas as pl
from jax.experimental.pallas import tpu as pltpu
from jax.sharding import Mesh
from jax.sharding import PartitionSpec as P

OWNER = ("owner_0", "owner_1", "owner_2")
AXES = ("section", "owner_0", "owner_1", "owner_2")
MESH = pl.DeviceIdType.MESH
F32 = jnp.float32
BF16 = jnp.bfloat16
ROWS = 16384
COLS = 32
CHUNK = 1024
NCHUNK = ROWS // CHUNK
BUILD = 4096
AUX = 168
NT = (((1,), (1,)), ((), ()))


def remote(src, dst, ssem, rsem, dev):
    return pltpu.make_async_remote_copy(
        src_ref=src, dst_ref=dst, send_sem=ssem, recv_sem=rsem, device_id=dev, device_id_type=MESH
    )


def silu_add(v, u):
    h = 0.5 * u
    return (v + (h + h * jnp.tanh(h))).astype(BF16)


def build_table(s, bk_ref, bv_ref, store):
    sel = lax.broadcasted_iota(jnp.int32, (COLS, 128), 1) == (
        lax.broadcasted_iota(jnp.int32, (COLS, 128), 0) + s * COLS
    )
    sel = sel.astype(F32).astype(BF16)
    total = jnp.zeros((256, 256), F32)
    step = 1024
    for i in range(BUILD // step):
        vals = lax.dot_general(sel, bv_ref[pl.ds(i * step, step), :], NT, preferred_element_type=F32)
        key = bk_ref[:, pl.ds(i * step, step)]
        low = (key & 255).astype(F32).astype(BF16)
        high = key >> 8
        hot = jnp.where(
            lax.broadcasted_iota(jnp.int32, (256, step), 0).astype(F32).astype(BF16) == low,
            jnp.ones((), BF16),
            jnp.zeros((), BF16),
        )
        wide = jnp.concatenate([jnp.where(high == p, vals, 0.0) for p in range(8)], axis=0)
        total += lax.dot_general(wide.astype(BF16), hot, NT, preferred_element_type=F32)
    store(total.astype(BF16))


def delta(e):
    return ((e + 1) // 2) * (2 * (e % 2) - 1)


def move_kernel(
    w_ref, v_ref, bk_ref, bv_ref, aux_ref, rbuf, tabs, auxg,
    sendbuf, wbuf, last, ws, wr, xs, xr, zs, zr, ys, yr, ls, lr, cs, cr, ps, pr, own_sem,
):
    s, z, y, c = [lax.axis_index(a) for a in AXES]

    def xdev(d):
        return (lax.rem(s + d, 4), z, y, c)

    def zdev(e):
        return (s, lax.rem(z + 8 + delta(e), 8), y, c)

    def ydev(d):
        return (s, z, lax.rem(y + 4 + d, 4), c)

    pair = (s, z, y, 1 - c)
    barrier = pltpu.get_barrier_semaphore()
    for d in (1, 2, 3):
        pl.semaphore_signal(barrier, inc=1, device_id=xdev(d), device_id_type=MESH)
    for e in range(1, 8):
        pl.semaphore_signal(barrier, inc=1, device_id=zdev(e), device_id_type=MESH)
    for d in (-1, 1):
        pl.semaphore_signal(barrier, inc=1, device_id=ydev(d), device_id_type=MESH)
    pl.semaphore_signal(barrier, inc=1, device_id=pair, device_id_type=MESH)
    pl.semaphore_wait(barrier, 13)

    def wcopy(d):
        return remote(w_ref, wbuf.at[s], ws.at[d], wr.at[d], xdev(d))

    def xcopy(d):
        return remote(aux_ref, auxg.at[s], xs.at[d], xr.at[d], xdev(d))

    def zfrom(e):
        return lax.rem(z + 8 - delta(e), 8)

    def zcopy(e):
        here = tabs.at[c, z, y]
        return remote(here, here, zs.at[e], zr.at[e], zdev(e))

    def ycopy(k, e):
        here = tabs.at[c, zfrom(e), y]
        return remote(here, here, ys.at[k, e], yr.at[k, e], ydev(1 - 2 * k))

    def lcopy(e):
        sign = 1 - 2 * (e % 2)
        here = tabs.at[c, zfrom(e), lax.rem(y + 4 - sign, 4)]
        return remote(here, here, ls.at[e], lr.at[e], ydev(sign))

    def ccopy(k, e):
        at = (0, -1, 1, 2)[k]
        here = tabs.at[c, zfrom(e), lax.rem(y + 4 + at, 4)]
        return remote(here, here, cs.at[k, e], cr.at[k, e], pair)

    def carrive(k, e):
        at = (0, -1, 1, 2)[k]
        here = tabs.at[1 - c, zfrom(e), lax.rem(y + 4 + at, 4)]
        return remote(here, here, cs.at[k, e], cr.at[k, e], pair)

    def pcopy(d, i):
        at = pl.ds(pl.multiple_of(i * CHUNK, CHUNK), CHUNK)
        return remote(
            sendbuf.at[lax.rem(s + d, 4), :, at], rbuf.at[s, :, at], ps.at[d, i], pr.at[d, i], xdev(d)
        )

    for d in (1, 3, 2):
        wcopy(d).start()
    for d in (1, 3, 2):
        xcopy(d).start()
    own_aux = pltpu.make_async_copy(aux_ref, auxg.at[s], own_sem.at[0])
    own_aux.start()
    own_w = pltpu.make_async_copy(w_ref, wbuf.at[s], own_sem.at[1])
    own_w.start()

    def put_table(value):
        tabs[c, z, y] = value

    build_table(s, bk_ref, bv_ref, put_table)

    own_w.wait()
    for d in (1, 2, 3):
        wcopy(d).wait_recv()
    w_last = wbuf[lax.rem(s + 3, 4)].astype(F32).T.astype(BF16)
    last[pl.ds(0, 128), :] = w_last
    eye = lax.broadcasted_iota(jnp.int32, (128, 128), 0) == lax.broadcasted_iota(jnp.int32, (128, 128), 1)
    last[pl.ds(128, 128), :] = eye.astype(F32).astype(BF16)

    def sections(i):
        at = pl.ds(pl.multiple_of(i * CHUNK, CHUNK), CHUNK)
        v = v_ref[at, :]
        for j in range(3):
            u = jnp.dot(v, wbuf[lax.rem(s + j, 4)], preferred_element_type=F32)
            v = silu_add(v.astype(F32), u)
        out = lax.dot_general(last[...], v, NT, preferred_element_type=F32)
        v = silu_add(out[128:], out[:128])
        for q in range(4):
            sendbuf[q, :, at] = v[q * COLS : (q + 1) * COLS]

    sections(0)
    for e in range(1, 8):
        zcopy(e).start()
    for k in (0, 1):
        ycopy(k, 0).start()
    ccopy(0, 0).start()

    def step(i, carry):
        sections(i)
        for d in (1, 3, 2):
            pcopy(d, i - 1).start()

        @pl.when((i >= 2) & (i % 2 == 0))
        def _():
            e = i // 2
            zcopy(e).wait_recv()
            for k in (0, 1):
                ycopy(k, e).start()
            ccopy(0, e).start()

        return carry

    lax.fori_loop(1, NCHUNK, step, 0)
    own_p = pltpu.make_async_copy(sendbuf.at[s], rbuf.at[s], own_sem.at[2])
    own_p.start()
    for d in (1, 3, 2):
        pcopy(d, NCHUNK - 1).start()

    def near(e, carry):
        ycopy(0, e).wait_recv()
        ycopy(1, e).wait_recv()
        lcopy(e).start()
        ccopy(1, e).start()
        ccopy(2, e).start()
        return carry

    lax.fori_loop(0, 8, near, 0)

    def far(e, carry):
        lcopy(e).wait_recv()
        ccopy(3, e).start()
        return carry

    lax.fori_loop(0, 8, far, 0)

    def finish(e, carry):
        for k in range(4):
            carrive(k, e).wait_recv()
            ccopy(k, e).wait_send()
        for k in (0, 1):
            ycopy(k, e).wait_send()
        lcopy(e).wait_send()
        return carry

    lax.fori_loop(0, 8, finish, 0)

    def finish_z(e, carry):
        zcopy(e).wait_send()
        return carry

    lax.fori_loop(1, 8, finish_z, 0)

    def finish_p(i, carry):
        for d in (1, 2, 3):
            pcopy(d, i).wait()
        return carry

    lax.fori_loop(0, NCHUNK, finish_p, 0)
    for d in (1, 2, 3):
        wcopy(d).wait_send()
        xcopy(d).wait()
    own_aux.wait()
    own_p.wait()


def move(w, v, bk, bv, aux):
    dma = pltpu.SemaphoreType.DMA
    vmem = pl.BlockSpec(memory_space=pltpu.VMEM)
    return pl.pallas_call(
        move_kernel,
        name="move",
        out_shape=(
            jax.ShapeDtypeStruct((4, COLS, ROWS), BF16),
            jax.ShapeDtypeStruct((2, 8, 4, 256, 256), BF16),
            jax.ShapeDtypeStruct((4, AUX, 128), jnp.int32),
        ),
        in_specs=[vmem] * 5,
        out_specs=(vmem, vmem, vmem),
        scratch_shapes=[
            pltpu.VMEM((4, COLS, ROWS), BF16),
            pltpu.VMEM((4, 128, 128), BF16),
            pltpu.VMEM((256, 128), BF16),
            dma((4,)), dma((4,)), dma((4,)), dma((4,)),
            dma((8,)), dma((8,)),
            dma((2, 8)), dma((2, 8)), dma((8,)), dma((8,)),
            dma((4, 8)), dma((4, 8)),
            dma((4, NCHUNK)), dma((4, NCHUNK)),
            dma((3,)),
        ],
        compiler_params=pltpu.CompilerParams(
            collective_id=0, has_side_effects=True, vmem_limit_bytes=60 << 20
        ),
    )(w, v, bk, bv, aux)


def join_kernel(where_ref, code_ref, pay_ref, tab_ref, acc_ref):
    i = pl.program_id(0)

    @pl.when(i == 0)
    def _():
        acc_ref[...] = jnp.zeros_like(acc_ref)

    one, zero = jnp.ones((), BF16), jnp.zeros((), BF16)
    code = code_ref[0]
    low = (code & 255).astype(F32).astype(BF16)
    high = (code >> 8) & 7
    glow = (code >> 11) & 7
    ghigh = (code >> 14).astype(F32).astype(BF16)
    rows256 = lax.broadcasted_iota(jnp.int32, (256, 128), 0).astype(F32).astype(BF16)
    rows128 = lax.broadcasted_iota(jnp.int32, (128, 128), 0).astype(F32).astype(BF16)
    wide, hots = [], []
    for b in range(CHUNK // 128):
        at = slice(b * 128, (b + 1) * 128)
        hot = jnp.where(rows256 == low[:, at], one, zero)
        table = tab_ref[where_ref[i * (CHUNK // 128) + b]]
        out = jnp.dot(table, hot, preferred_element_type=F32)
        matched = jnp.zeros((COLS, 128), F32)
        for p in range(8):
            matched = jnp.where(high[:, at] == p, out[p * COLS : (p + 1) * COLS], matched)
        joined = pay_ref[0, :, at].astype(F32) * matched
        wide.append(
            jnp.concatenate(
                [jnp.where(glow[:, at] == p, joined, 0.0).astype(BF16) for p in range(8)], axis=0
            )
        )
        hots.append(jnp.where(rows128 == ghigh[:, at], one, zero))
    acc_ref[...] += lax.dot_general(
        jnp.concatenate(hots, axis=1), jnp.concatenate(wide, axis=1), NT, preferred_element_type=F32
    )


def join(where, code, pay, tabs):
    n = 4 * NCHUNK
    return pl.pallas_call(
        join_kernel,
        name="join",
        out_shape=jax.ShapeDtypeStruct((128, 256), F32),
        grid_spec=pltpu.PrefetchScalarGridSpec(
            num_scalar_prefetch=1,
            grid=(n,),
            in_specs=[
                pl.BlockSpec((1, 1, CHUNK), lambda i, w: (i, 0, 0)),
                pl.BlockSpec((1, COLS, CHUNK), lambda i, w: (i // NCHUNK, 0, i % NCHUNK)),
                pl.BlockSpec((64, 256, 256), lambda i, w: (0, 0, 0), pipeline_mode=pl.Buffered(1)),
            ],
            out_specs=pl.BlockSpec((128, 256), lambda i, w: (0, 0)),
        ),
        compiler_params=pltpu.CompilerParams(
            dimension_semantics=("arbitrary",), vmem_limit_bytes=40 << 20
        ),
    )(where, code, pay, tabs)


def reduce_kernel(acc_ref, out_ref, first, mid, second, s1, r1, s2, r2):
    s, z, y, c = [lax.axis_index(a) for a in AXES]
    me = s * 2 + c
    place = z * 4 + y

    def peer1(k):
        t = lax.rem(me + k, 8)
        return t // 2, lax.rem(t, 2)

    def dev2(k):
        t = lax.rem(place + k, 32)
        return (s, t // 4, lax.rem(t, 4), c)

    barrier = pltpu.get_barrier_semaphore()
    for k in range(1, 8):
        ps, pc = peer1(k)
        pl.semaphore_signal(barrier, inc=1, device_id=(ps, z, y, pc), device_id_type=MESH)

    def greet(k, carry):
        pl.semaphore_signal(barrier, inc=1, device_id=dev2(k), device_id_type=MESH)
        return carry

    lax.fori_loop(1, 32, greet, 0)
    pl.semaphore_wait(barrier, 38)

    def piece(ps, pc):
        return (
            pl.ds(pl.multiple_of(ps * 32, 32), 32),
            pl.ds(pl.multiple_of(pc * 128, 128), 128),
        )

    def copy1(k):
        ps, pc = peer1(k)
        rows, lanes = piece(ps, pc)
        return remote(acc_ref.at[rows, lanes], first.at[me], s1.at[k], r1.at[k], (ps, z, y, pc))

    def copy2(k):
        return remote(
            mid.at[lax.rem(place + k, 32)], second.at[place], s2.at[k], r2.at[k], dev2(k)
        )

    for k in range(1, 8):
        copy1(k).start()
    rows, lanes = piece(s, c)
    first[me] = acc_ref[rows, lanes]
    for k in range(1, 8):
        copy1(k).wait_recv()
    for x in range(4):
        mid[:, x, :] = first[2 * x] + first[2 * x + 1]

    def send(k, carry):
        copy2(k).start()
        return carry

    lax.fori_loop(1, 32, send, 0)
    second[place] = mid[place]

    def take(k, carry):
        copy2(k).wait_recv()
        return carry

    lax.fori_loop(1, 32, take, 0)
    out_ref[...] = jnp.sum(second[...], axis=0)
    for k in range(1, 8):
        copy1(k).wait_send()

    def done(k, carry):
        copy2(k).wait_send()
        return carry

    lax.fori_loop(1, 32, done, 0)


def reduce_all(acc):
    dma = pltpu.SemaphoreType.DMA
    vmem = pl.BlockSpec(memory_space=pltpu.VMEM)
    return pl.pallas_call(
        reduce_kernel,
        name="reduce_all",
        out_shape=jax.ShapeDtypeStruct((4, 128), F32),
        in_specs=[vmem],
        out_specs=vmem,
        scratch_shapes=[
            pltpu.VMEM((8, 32, 128), F32),
            pltpu.VMEM((32, 4, 128), F32),
            pltpu.VMEM((32, 4, 128), F32),
            dma((8,)), dma((8,)), dma((32,)), dma((32,)),
        ],
        compiler_params=pltpu.CompilerParams(
            collective_id=1, has_side_effects=True, vmem_limit_bytes=16 << 20
        ),
    )(acc)


def local(probe_values, probe_keys, group_ids, block_dest, filter_bits, section_weights, build_keys, build_values):
    code = (probe_keys | (group_ids << 11)).reshape(128, 128)
    aux = jnp.concatenate(
        [
            code,
            filter_bits.reshape(32, 128),
            jnp.broadcast_to(block_dest.reshape(1, 128), (8, 128)),
        ],
        axis=0,
    )
    rbuf, tabs, auxg = move(
        section_weights[0], probe_values.reshape(ROWS, 128), build_keys.reshape(1, BUILD), build_values, aux
    )
    bits = auxg[:, 128:160].reshape(4, 8, 512)
    bits = bits[0] & bits[1] & bits[2] & bits[3]
    kept = (bits[..., None] >> jnp.arange(16, dtype=jnp.int32)) & 1
    code = auxg[:, :128].reshape(4 * NCHUNK, 1, CHUNK)
    code = jnp.where(kept.reshape(code.shape) == 1, code, code | (1 << 21))
    dest = auxg[:, 160].reshape(512)
    where = (dest & 1) * 32 + (dest >> 3) * 4 + ((dest >> 1) & 3)
    acc = join(where, code, rbuf, tabs.reshape(64, 256, 256))
    out = reduce_all(acc)
    return out.reshape(4, 4, COLS).transpose(1, 0, 2).reshape(4, 128)


def solution(mesh):
    torus = Mesh(mesh.devices.reshape(mesh.shape["section"], 8, 4, 2), AXES)
    return jax.shard_map(
        local,
        mesh=torus,
        in_specs=(
            P("section", OWNER, None),
            P("section", OWNER),
            P("section", OWNER),
            P("section", OWNER, None),
            P("section", None, OWNER),
            P("section", None, None),
            P(OWNER),
            P(OWNER, None),
        ),
        out_specs=P(AXES, None),
        check_vma=False,
    )
```

time: 518 us -> 152 us (0.29)
  waiting for transfers between devices: 162 us -> 0 us
  Pallas kernels: 0 us -> 136 us
  local copies, waits for them, and re-layouts: 145 us -> 9.51 us
  matrix products: 97.6 us -> 0 us
  starting transfers between devices: 44.5 us -> 0 us
  blocking collectives: 29.9 us -> 0 us
  other arithmetic: 34.9 us -> 5.56 us
    all_to_all x5 -> x0, waiting for transfers between devices: 162 us -> none  [the longest x1 159 us: local(): lax.all_to_all(send_values, OWNER, split_axis=1, concat_axis=1, tiled=True)]
    pallas_call x0 -> x3, Pallas kernels: none -> 136 us  [the longest x1 69.1 us: move(): pl.pallas_call(move_kernel, name='move', out_shape=(jax.ShapeDtypeStruct(...]
    gather x19 -> x0, local copies, waits for them, and re-layouts: 102 us -> none  [the longest x16 87.4 us: add_block(): matched = jnp.take(key_table, part_keys, axis=0)]
    dot_general x20 -> x0, matrix products: 97.6 us -> none  [the longest x16 66.1 us: add_block(): lax.dot_general(onehot, joined, (((0,), (0,)), ((), ())), preferred_eleme...]
    all_to_all x5 -> x0, starting transfers between devices: 44.5 us -> none  [the longest x1 14.3 us: local(): lax.all_to_all(send_keys, OWNER, split_axis=1, concat_axis=1, tiled=True)]
    all_to_all x2 -> x0, blocking collectives: 29.9 us -> none  [the longest x1 17.1 us: summed_on_arrival(): pieces = lax.all_to_all(cut_along(x, dim, size), axis, 0, 0, tiled=True)]
    scatter-add x1 -> x0, other arithmetic: 22.8 us -> none  [local(): jax.ops.segment_sum(build_values.astype(jnp.float32), build_keys, num_seg...]
    select_n x1 -> x0, local copies, waits for them, and re-layouts: 10.3 us -> none  [pick_blocks(): jnp.take(table_rows, picks.reshape(-1), axis=0)]
  transfers between devices with their start and end apart: 5 -> 0, of which waited for: 2 -> 0; matrix products, arithmetic and copies ran while one was open for 21% -> 0% of each run, Pallas kernels for 0% -> 0%
where the time goes in v1:
time: 152 us; the launch traced here: 151 us
  Pallas kernels  136 us (89%)
  local copies, waits for them, and re-layouts  9.51 us (6%)
  other arithmetic  5.56 us (4%)
    pallas_call x1, Pallas kernels, move(): pl.pallas_call(move_kernel, name='move', out_shape=(jax.ShapeDtypeStruct(...  69.1 us
    pallas_call x1, Pallas kernels, join(): pl.pallas_call(join_kernel, name='join', out_shape=jax.ShapeDtypeStruct((...  48.9 us
    pallas_call x1, Pallas kernels, reduce_all(): pl.pallas_call(reduce_kernel, name='reduce_all', out_shape=jax.ShapeDtype...  18.3 us
    unnamed x5, local copies, waits for them, and re-layouts  6.07 us

profile of v1, /device:TPU:1, one launch (start us, length us, event | category | flops | bytes accessed | tf_op | source)
XLA Modules:
  0.0 151.4 jit_solution(14263006439696699199)
XLA Ops:
  0.0 0.5 broadcast.53
  0.5 1.3 reduce.3
  1.9 0.1 broadcast_in_dim.4
  1.9 0.7 reshape.131
  2.7 0.9 shift-left_or_fusion
  3.6 0.1 reshape.130
  3.6 0.6 pad_add_fusion.aux_ref
  4.3 69.1 %move.1 = (bf16[4,32,16384]{2,1,0:T(8,128)(2,1)}, bf16[2,8,4,256,256]{4,3,2,1,0:T(8,128)(2,1)}, s32[4,168,128]{2,1,0:T(8,128)}) custom-call(bf16[128,128]{1,0:T(8,128)(2,1)} %bitcast.13, bf16[16384,128]{1,0:T(8,128)(2,1)} %bitcast.11, s32[1,4096]{1,0:T(1,128)} %bitcast.15, bf16[4096,128]{1,0:T(8,128)(2,1)} %bv_ref.1, s32[168,128]{1,0:T(8,128)} %pad_add_fusion.aux_ref), custom_call_target="tpu_custom_call" | custom-call | tf_op jit(solution)/shard_map/move/pallas_call | solution.py:237
  73.4 0.7 and_add_fusion
  74.1 0.8 slice_and_fusion
  74.9 1.0 slice.32
  75.9 0.7 and_compare_fusion
  76.6 0.8 eq.17
  77.5 0.4 or_select_fusion.code_ref
  77.9 0.0 copy-start
  77.9 3.4 %copy-done = bf16[2,8,4,256,256]{4,3,2,1,0:T(8,128)(2,1)S(1)} copy-done((bf16[2,8,4,256,256]{4,3,2,1,0:T(8,128)(2,1)S(1)}, bf16[2,8,4,256,256]{4,3,2,1,0:T(8,128)(2,1)}, u32[]{:S(2)}) %copy-start) | copy-done | bytes 8388632
  81.3 0.0 copy-start.1
  81.3 2.2 %copy-done.1 = bf16[4,32,16384]{2,1,0:T(8,128)(2,1)S(1)} copy-done((bf16[4,32,16384]{2,1,0:T(8,128)(2,1)S(1)}, bf16[4,32,16384]{2,1,0:T(8,128)(2,1)}, u32[]{:S(2)}) %copy-start.1) | copy-done | bytes 4194328
  83.5 48.9 %join.1.acc_ref = f32[128,256]{1,0:T(8,128)S(1)} custom-call(s32[512]{0:T(512)S(1)} %bitcast.10, s32[64,1,1024]{2,1,0:T(1,128)S(1)} %or_select_fusion.code_ref, bf16[4,32,16384]{2,1,0:T(8,128)(2,1)S(1)} %copy-done.1, bf16[64,256,256]{2,1,0:T(8,128)(2,1)S(1)} %bitcast.9), custom_call_target="tpu_custom_call" | custom-call | tf_op jit(solution)/shard_map/join/pallas_call | solution.py:302
  132.4 18.3 %reduce_all.1 = f32[4,128]{1,0:T(4,128)S(1)} custom-call(f32[128,256]{1,0:T(8,128)S(1)} %join.1.acc_ref), custom_call_target="tpu_custom_call" | custom-call | tf_op jit(solution)/shard_map/reduce_all/pallas_call | solution.py:398
  150.7 0.1 reshape.134
  150.8 0.7 reshape.135
  (4 shorter events, 0.0 us)
Async XLA Ops:
  77.9 3.4 %copy-start = (bf16[2,8,4,256,256]{4,3,2,1,0:T(8,128)(2,1)S(1)}, bf16[2,8,4,256,256]{4,3,2,1,0:T(8,128)(2,1)}, u32[]{:S(2)}) copy-start(bf16[2,8,4,256,256]{4,3,2,1,0:T(8,128)(2,1)} %get-tuple-element.10) | copy-start | bytes 25165828
  81.3 2.2 %copy-start.1 = (bf16[4,32,16384]{2,1,0:T(8,128)(2,1)S(1)}, bf16[4,32,16384]{2,1,0:T(8,128)(2,1)}, u32[]{:S(2)}) copy-start(bf16[4,32,16384]{2,1,0:T(8,128)(2,1)} %get-tuple-element.9.pay_ref) | copy-start | bytes 12582916

commit v2 on v1

v2 whole, which is shorter than its diff:
```python
import functools

import jax
import jax.numpy as jnp
from jax import lax
from jax.experimental import pallas as pl
from jax.experimental.pallas import tpu as pltpu
from jax.sharding import Mesh
from jax.sharding import PartitionSpec as P

OWNER = ("owner_0", "owner_1", "owner_2")
AXES = ("section", "owner_0", "owner_1", "owner_2")
MESH = pl.DeviceIdType.MESH
F32 = jnp.float32
BF16 = jnp.bfloat16
ROWS = 16384
COLS = 32
CHUNK = 1024
NCHUNK = ROWS // CHUNK
BUILD = 4096
NT = (((1,), (1,)), ((), ()))


def remote(src, dst, ssem, rsem, dev):
    return pltpu.make_async_remote_copy(
        src_ref=src, dst_ref=dst, send_sem=ssem, recv_sem=rsem, device_id=dev, device_id_type=MESH
    )


def silu_add(v, u):
    h = 0.5 * u
    return (v + (h + h * jnp.tanh(h))).astype(BF16)


def build_table(s, bk_ref, bv_ref, store):
    sel = lax.broadcasted_iota(jnp.int32, (COLS, 128), 1) == (
        lax.broadcasted_iota(jnp.int32, (COLS, 128), 0) + s * COLS
    )
    sel = sel.astype(F32).astype(BF16)
    total = jnp.zeros((256, 256), F32)
    step = 1024
    for i in range(BUILD // step):
        vals = lax.dot_general(sel, bv_ref[pl.ds(i * step, step), :], NT, preferred_element_type=F32)
        key = bk_ref[:, pl.ds(i * step, step)]
        low = (key & 255).astype(F32).astype(BF16)
        high = key >> 8
        hot = jnp.where(
            lax.broadcasted_iota(jnp.int32, (256, step), 0).astype(F32).astype(BF16) == low,
            jnp.ones((), BF16),
            jnp.zeros((), BF16),
        )
        wide = jnp.concatenate([jnp.where(high == p, vals, 0.0) for p in range(8)], axis=0)
        total += lax.dot_general(wide.astype(BF16), hot, NT, preferred_element_type=F32)
    store(total.astype(BF16))


def delta(e):
    return ((e + 1) // 2) * (2 * (e % 2) - 1)


def fused_kernel(
    w_ref, v_hbm, key_ref, grp_ref, dst_ref, bit_ref, bk_ref, bv_ref, out_ref,
    vbuf, sendbuf, rbuf, tabs, wbuf, last, codes, codeg, bitg, dests, destg, where_ref, kept_ref,
    hot0, hot1, wide0, wide1, acc_ref, first, mid, second,
    vs, ws, wr, xs, xr, zs, zr, ys, yr, ls, lr, cs, cr, ps, pr, own_sem, s1, r1, s2, r2,
):
    s, z, y, c = [lax.axis_index(a) for a in AXES]
    me = s * 2 + c
    place = z * 4 + y

    def xdev(d):
        return (lax.rem(s + d, 4), z, y, c)

    def zdev(e):
        return (s, lax.rem(z + 8 + delta(e), 8), y, c)

    def ydev(d):
        return (s, z, lax.rem(y + 4 + d, 4), c)

    pair = (s, z, y, 1 - c)

    def peer1(k):
        t = lax.rem(me + k, 8)
        return t // 2, lax.rem(t, 2)

    def dev2(k):
        t = lax.rem(place + k, 32)
        return (s, t // 4, lax.rem(t, 4), c)

    barrier = pltpu.get_barrier_semaphore()
    for k in range(1, 8):
        px, pc = peer1(k)
        pl.semaphore_signal(barrier, inc=1, device_id=(px, z, y, pc), device_id_type=MESH)

    def greet(k, carry):
        pl.semaphore_signal(barrier, inc=1, device_id=dev2(k), device_id_type=MESH)
        return carry

    lax.fori_loop(1, 32, greet, 0)

    def vcopy(i):
        at = pl.ds(pl.multiple_of(i * CHUNK, CHUNK), CHUNK)
        return pltpu.make_async_copy(v_hbm.at[at, :], vbuf.at[at, :], vs.at[i])

    def vstart(i, carry):
        vcopy(i).start()
        return carry

    lax.fori_loop(0, NCHUNK, vstart, 0)

    for i in range(NCHUNK):
        at = slice((i % 8) * CHUNK, (i % 8 + 1) * CHUNK)
        m = slice(i // 8, i // 8 + 1)
        codes[i : i + 1, :] = key_ref[m, at] | (grp_ref[m, at] << 11)
    d = dst_ref[...]
    dests[...] = jnp.zeros_like(dests)
    dests[0:2, 0:64] = (d & 1) * 32 + (d >> 3) * 4 + ((d >> 1) & 3)

    def wcopy(d):
        return remote(w_ref, wbuf.at[s], ws.at[d], wr.at[d], xdev(d))

    def xcopies(d):
        return [
            remote(a, b.at[s], xs.at[n, d], xr.at[n, d], xdev(d))
            for n, (a, b) in enumerate(((codes, codeg), (bit_ref, bitg), (dests, destg)))
        ]

    def slot(cc, zz, yy):
        return cc * 32 + zz * 4 + yy

    def zfrom(e):
        return lax.rem(z + 8 - delta(e), 8)

    def zcopy(e):
        here = tabs.at[slot(c, z, y)]
        return remote(here, here, zs.at[e], zr.at[e], zdev(e))

    def ycopy(k, e):
        here = tabs.at[slot(c, zfrom(e), y)]
        return remote(here, here, ys.at[k, e], yr.at[k, e], ydev(1 - 2 * k))

    def lcopy(e):
        sign = 1 - 2 * (e % 2)
        here = tabs.at[slot(c, zfrom(e), lax.rem(y + 4 - sign, 4))]
        return remote(here, here, ls.at[e], lr.at[e], ydev(sign))

    def ccopy(k, e):
        at = (0, -1, 1, 2)[k]
        here = tabs.at[slot(c, zfrom(e), lax.rem(y + 4 + at, 4))]
        return remote(here, here, cs.at[k, e], cr.at[k, e], pair)

    def carrive(k, e):
        at = (0, -1, 1, 2)[k]
        here = tabs.at[slot(1 - c, zfrom(e), lax.rem(y + 4 + at, 4))]
        return remote(here, here, cs.at[k, e], cr.at[k, e], pair)

    def pcopy(d, i):
        at = pl.ds(pl.multiple_of(i * CHUNK, CHUNK), CHUNK)
        return remote(
            sendbuf.at[lax.rem(s + d, 4), :, at], rbuf.at[s, :, at], ps.at[d, i], pr.at[d, i], xdev(d)
        )

    def put_table(value):
        tabs[slot(c, z, y)] = value

    build_table(s, bk_ref, bv_ref, put_table)
    pl.semaphore_wait(barrier, 38)

    for d in (1, 3, 2):
        wcopy(d).start()
    for e in range(1, 8):
        zcopy(e).start()
    for k in (0, 1):
        ycopy(k, 0).start()
    ccopy(0, 0).start()
    for d in (1, 3, 2):
        for cp in xcopies(d):
            cp.start()
    own = [
        pltpu.make_async_copy(a, b.at[s], own_sem.at[n])
        for n, (a, b) in enumerate(((codes, codeg), (bit_ref, bitg), (dests, destg), (w_ref, wbuf)))
    ]
    for cp in own:
        cp.start()
    for cp in own:
        cp.wait()
    for d in (1, 2, 3):
        wcopy(d).wait_recv()
    w_last = wbuf[lax.rem(s + 3, 4)].astype(F32).T.astype(BF16)
    last[pl.ds(0, 128), :] = w_last
    eye = lax.broadcasted_iota(jnp.int32, (128, 128), 0) == lax.broadcasted_iota(jnp.int32, (128, 128), 1)
    last[pl.ds(128, 128), :] = eye.astype(F32).astype(BF16)

    def sections(i):
        at = pl.ds(pl.multiple_of(i * CHUNK, CHUNK), CHUNK)
        vcopy(i).wait()
        v = vbuf[at, :]
        for j in range(3):
            u = jnp.dot(v, wbuf[lax.rem(s + j, 4)], preferred_element_type=F32)
            v = silu_add(v.astype(F32), u)
        out = lax.dot_general(last[...], v, NT, preferred_element_type=F32)
        v = silu_add(out[128:], out[:128])
        for q in range(4):
            sendbuf[q, :, at] = v[q * COLS : (q + 1) * COLS]

    sections(0)

    def step(i, carry):
        sections(i)
        for d in (1, 3, 2):
            pcopy(d, i - 1).start()

        @pl.when(i % 2 == 1)
        def _():
            @pl.when(i < 14)
            def _():
                e = i // 2 + 1
                zcopy(e).wait_recv()
                for k in (0, 1):
                    ycopy(k, e).start()
                ccopy(0, e).start()

        return carry

    lax.fori_loop(1, NCHUNK, step, 0)
    own_p = pltpu.make_async_copy(sendbuf.at[s], rbuf.at[s], own_sem.at[4])
    own_p.start()
    for d in (1, 3, 2):
        pcopy(d, NCHUNK - 1).start()

    for d in (1, 2, 3):
        for cp in xcopies(d):
            cp.wait_recv()
    to_scalar = pltpu.make_async_copy(destg, where_ref, own_sem.at[5])
    to_scalar.start()
    words = bitg[0] & bitg[1] & bitg[2] & bitg[3]
    parts = jnp.concatenate([words & 255, words >> 8], axis=0).astype(F32).astype(BF16)
    shift = lax.broadcasted_iota(jnp.int32, (8, CHUNK), 1) & 15
    wide_iota = lax.broadcasted_iota(jnp.int32, (512, CHUNK), 1) >> 4
    word_iota = lax.broadcasted_iota(jnp.int32, (512, CHUNK), 0)
    for k in range(8):
        spread = (wide_iota + k * 64 == word_iota).astype(F32).astype(BF16)
        got = jnp.dot(parts, spread, preferred_element_type=F32).astype(jnp.int32)
        kept_ref[k] = ((got[:8] + got[8:] * 256) >> shift) & 1
    to_scalar.wait()
    own_p.wait()
    acc_ref[...] = jnp.zeros_like(acc_ref)
    hot1[...] = jnp.zeros_like(hot1)
    wide1[...] = jnp.zeros_like(wide1)

    def near(e, carry):
        ycopy(0, e).wait_recv()
        ycopy(1, e).wait_recv()
        lcopy(e).start()
        ccopy(1, e).start()
        ccopy(2, e).start()
        return carry

    lax.fori_loop(0, 8, near, 0)

    def far(e, carry):
        lcopy(e).wait_recv()
        ccopy(3, e).start()
        return carry

    lax.fori_loop(0, 8, far, 0)

    def finish(e, carry):
        for k in range(4):
            carrive(k, e).wait_recv()
        return carry

    lax.fori_loop(0, 8, finish, 0)

    one, zero = jnp.ones((), BF16), jnp.zeros((), BF16)
    rows256 = lax.broadcasted_iota(jnp.int32, (256, 128), 0).astype(F32).astype(BF16)
    rows128 = lax.broadcasted_iota(jnp.int32, (128, 128), 0).astype(F32).astype(BF16)

    def gather(src, i, hot_ref, wide_ref):
        code = codeg[src, pl.ds(i, 1), :]
        kept = kept_ref[i % 8, pl.ds(2 * src + i // 8, 1), :]
        low = (code & 255).astype(F32).astype(BF16)
        high = (code >> 8) & 7
        glow = (code >> 11) & 7
        ghigh = jnp.where(kept == 1, code >> 14, -1).astype(F32).astype(BF16)
        for b in range(CHUNK // 128):
            at = slice(b * 128, (b + 1) * 128)
            hot = jnp.where(rows256 == low[:, at], one, zero)
            table = tabs[where_ref[src, i // 8, (i % 8) * 8 + b]]
            out = jnp.dot(table, hot, preferred_element_type=F32)
            matched = jnp.zeros((COLS, 128), F32)
            for p in range(8):
                matched = jnp.where(high[:, at] == p, out[p * COLS : (p + 1) * COLS], matched)
            pay = rbuf[src, :, pl.ds(pl.multiple_of(i * CHUNK + b * 128, 128), 128)]
            joined = pay.astype(F32) * matched
            for p in range(8):
                wide_ref[p * COLS : (p + 1) * COLS, at] = jnp.where(glow[:, at] == p, joined, 0.0).astype(BF16)
            hot_ref[:, at] = jnp.where(rows128 == ghigh[:, at], one, zero)

    def group(hot_ref, wide_ref):
        acc_ref[...] += lax.dot_general(hot_ref[...], wide_ref[...], NT, preferred_element_type=F32)

    def join(t, carry):
        d = t % 4
        i = t // 4 * 2
        src = lax.rem(s + 4 - d, 4)

        @pl.when(d > 0)
        def _():
            pcopy(d, i).wait_recv()
            pcopy(d, i + 1).wait_recv()

        group(hot1, wide1)
        gather(src, i, hot0, wide0)
        group(hot0, wide0)
        gather(src, i + 1, hot1, wide1)
        return carry

    lax.fori_loop(0, 32, join, 0)
    group(hot1, wide1)

    def piece(px, pc):
        return (
            pl.ds(pl.multiple_of(px * 32, 32), 32),
            pl.ds(pl.multiple_of(pc * 128, 128), 128),
        )

    def copy1(k):
        px, pc = peer1(k)
        rows, lanes = piece(px, pc)
        return remote(acc_ref.at[rows, lanes], first.at[me], s1.at[k], r1.at[k], (px, z, y, pc))

    def copy2(k):
        return remote(mid.at[lax.rem(place + k, 32)], second.at[place], s2.at[k], r2.at[k], dev2(k))

    for k in range(1, 8):
        copy1(k).start()
    rows, lanes = piece(s, c)
    first[me] = acc_ref[rows, lanes]

    def sent_e(e, carry):
        for k in range(4):
            ccopy(k, e).wait_send()
        for k in (0, 1):
            ycopy(k, e).wait_send()
        lcopy(e).wait_send()
        return carry

    lax.fori_loop(0, 8, sent_e, 0)

    def sent_z(e, carry):
        zcopy(e).wait_send()
        return carry

    lax.fori_loop(1, 8, sent_z, 0)

    def sent_p(i, carry):
        for d in (1, 2, 3):
            pcopy(d, i).wait_send()
        return carry

    lax.fori_loop(0, NCHUNK, sent_p, 0)
    for d in (1, 2, 3):
        wcopy(d).wait_send()
        for cp in xcopies(d):
            cp.wait_send()

    for k in range(1, 8):
        copy1(k).wait_recv()
    for x in range(4):
        mid[:, x, :] = first[2 * x] + first[2 * x + 1]

    def send(k, carry):
        copy2(k).start()
        return carry

    lax.fori_loop(1, 32, send, 0)
    second[place] = mid[place]

    def take(k, carry):
        copy2(k).wait_recv()
        return carry

    lax.fori_loop(1, 32, take, 0)
    total = jnp.sum(second[...], axis=0)
    for x in range(4):
        for k in range(4):
            out_ref[k : k + 1, x * COLS : (x + 1) * COLS] = total[x : x + 1, k * COLS : (k + 1) * COLS]
    for k in range(1, 8):
        copy1(k).wait_send()

    def done(k, carry):
        copy2(k).wait_send()
        return carry

    lax.fori_loop(1, 32, done, 0)


def local(probe_values, probe_keys, group_ids, block_dest, filter_bits, section_weights, build_keys, build_values):
    dma = pltpu.SemaphoreType.DMA
    vmem = pl.BlockSpec(memory_space=pltpu.VMEM)
    i32 = jnp.int32
    return pl.pallas_call(
        fused_kernel,
        name="fused",
        out_shape=jax.ShapeDtypeStruct((4, 128), F32),
        in_specs=[vmem, pl.BlockSpec(memory_space=pl.ANY)] + [vmem] * 6,
        out_specs=vmem,
        scratch_shapes=[
            pltpu.VMEM((ROWS, 128), BF16),
            pltpu.VMEM((4, COLS, ROWS), BF16),
            pltpu.VMEM((4, COLS, ROWS), BF16),
            pltpu.VMEM((64, 256, 256), BF16),
            pltpu.VMEM((4, 128, 128), BF16),
            pltpu.VMEM((256, 128), BF16),
            pltpu.VMEM((NCHUNK, CHUNK), i32),
            pltpu.VMEM((4, NCHUNK, CHUNK), i32),
            pltpu.VMEM((4, 8, 512), i32),
            pltpu.VMEM((8, 128), i32),
            pltpu.VMEM((4, 8, 128), i32),
            pltpu.SMEM((4, 8, 128), i32),
            pltpu.VMEM((8, 8, CHUNK), i32),
            pltpu.VMEM((128, CHUNK), BF16),
            pltpu.VMEM((128, CHUNK), BF16),
            pltpu.VMEM((256, CHUNK), BF16),
            pltpu.VMEM((256, CHUNK), BF16),
            pltpu.VMEM((128, 256), F32),
            pltpu.VMEM((8, 32, 128), F32),
            pltpu.VMEM((32, 4, 128), F32),
            pltpu.VMEM((32, 4, 128), F32),
            dma((NCHUNK,)),
            dma((4,)), dma((4,)), dma((3, 4)), dma((3, 4)),
            dma((8,)), dma((8,)),
            dma((2, 8)), dma((2, 8)), dma((8,)), dma((8,)),
            dma((4, 8)), dma((4, 8)),
            dma((4, NCHUNK)), dma((4, NCHUNK)),
            dma((6,)),
            dma((8,)), dma((8,)), dma((32,)), dma((32,)),
        ],
        compiler_params=pltpu.CompilerParams(
            collective_id=0, has_side_effects=True, vmem_limit_bytes=60 << 20
        ),
    )(
        section_weights[0],
        probe_values.reshape(ROWS, 128),
        probe_keys,
        group_ids,
        block_dest.reshape(2, 64),
        filter_bits[0],
        build_keys.reshape(1, BUILD),
        build_values,
    )


def solution(mesh):
    torus = Mesh(mesh.devices.reshape(mesh.shape["section"], 8, 4, 2), AXES)
    return jax.shard_map(
        local,
        mesh=torus,
        in_specs=(
            P("section", OWNER, None),
            P("section", OWNER),
            P("section", OWNER),
            P("section", OWNER, None),
            P("section", None, OWNER),
            P("section", None, None),
            P(OWNER),
            P(OWNER, None),
        ),
        out_specs=P(AXES, None),
        check_vma=False,
    )
```

time: 152 us -> 106 us (0.70)
  Pallas kernels: 136 us -> 105 us
  local copies, waits for them, and re-layouts: 9.51 us -> 1.26 us
  other arithmetic: 5.56 us -> 0 us
    pallas_call x3 -> x1, Pallas kernels: 136 us -> 105 us  [local(): pl.pallas_call(fused_kernel, name='fused', out_shape=jax.ShapeDtypeStruct...]
    unnamed x5 -> x1, local copies, waits for them, and re-layouts: 6.07 us -> 1.26 us
    reshape x4 -> x0, local copies, waits for them, and re-layouts: 1.53 us -> none  [the longest x2 0.75 us: local(): return out.reshape(4, 4, COLS).transpose(1, 0, 2).reshape(4, 128)]
where the time goes in v2:
time: 106 us
  Pallas kernels  105 us (99%)
  local copies, waits for them, and re-layouts  1.26 us (1%)
    pallas_call x1, Pallas kernels, local(): pl.pallas_call(fused_kernel, name='fused', out_shape=jax.ShapeDtypeStruct...  105 us

profile of v2, /device:TPU:1, one launch (start us, length us, event | category | flops | bytes accessed | tf_op | source)
XLA Modules:
  0.0 106.0 jit_solution(6820190123587327103)
XLA Ops:
  0.0 104.8 %fused.1 = f32[4,128]{1,0:T(4,128)} custom-call(bf16[128,128]{1,0:T(8,128)(2,1)} %bitcast.6, bf16[16384,128]{1,0:T(8,128)(2,1)} %bitcast.5, s32[2,8192]{1,0:T(2,128)} %key_ref.1, s32[2,8192]{1,0:T(2,128)} %grp_ref.1, s32[2,64]{1,0:T(2,128)} %bitcast.9, s32[8,512]{1,0:T(8,128)} %bitcast.7, s32[1,4096]{1,0:T(1,128)} %bitcast.8, bf16[4096,128]{1,0:T(8,128)(2,1)} %bv_ref.1), custom_call_target="tpu_custom_call" | custom-call | tf_op jit(solution)/shard_map/fused/pallas_call | solution.py:403
  104.8 1.3 %copy.10 = f32[4,128]{1,0:T(4,128)} copy(f32[4,128]{1,0:T(4,128)} %fused.1) | data formatting | bytes 4096

commit v3 on v2

--- a/solution.py
+++ b/solution.py
@@ -18,6 +18,10 @@
 CHUNK = 1024
 NCHUNK = ROWS // CHUNK
 BUILD = 4096
+PERMUTED = 4
+A_ROWS = 176
+HOPS = (4, 3)
+EVENTS = (None, (0, 1), (1, 1), (0, 2), (1, 2), (0, 3), (1, 3), (0, 4))
 NT = (((1,), (1,)), ((), ()))
 
 
@@ -27,8 +31,7 @@
     )
 
 
-def silu_add(v, u):
-    h = 0.5 * u
+def silu_add(v, h):
     return (v + (h + h * jnp.tanh(h))).astype(BF16)
 
 
@@ -54,15 +57,11 @@
     store(total.astype(BF16))
 
 
-def delta(e):
-    return ((e + 1) // 2) * (2 * (e % 2) - 1)
-
-
 def fused_kernel(
     w_ref, v_hbm, key_ref, grp_ref, dst_ref, bit_ref, bk_ref, bv_ref, out_ref,
-    vbuf, sendbuf, rbuf, tabs, wbuf, last, codes, codeg, bitg, dests, destg, where_ref, kept_ref,
-    hot0, hot1, wide0, wide1, acc_ref, first, mid, second,
-    vs, ws, wr, xs, xr, zs, zr, ys, yr, ls, lr, cs, cr, ps, pr, own_sem, s1, r1, s2, r2,
+    vbuf, sendbuf, rbuf, tabs, wbuf, half, last, codes, codeg, bitg, dests, destg, where_ref, kept_ref,
+    acc_ref, first, mid, second,
+    vs, ws, wr, xs, xr, azs, azr, bzs, bzr, bys, byr, ys, yr, ls, lr, cs, cr, cbs, cbr, ps, pr, own_sem, s1, r1, s2, r2,
 ):
     s, z, y, c = [lax.axis_index(a) for a in AXES]
     me = s * 2 + c
@@ -71,9 +70,6 @@
     def xdev(d):
         return (lax.rem(s + d, 4), z, y, c)
 
-    def zdev(e):
-        return (s, lax.rem(z + 8 + delta(e), 8), y, c)
-
     def ydev(d):
         return (s, z, lax.rem(y + 4 + d, 4), c)
 
@@ -107,6 +103,124 @@
         return carry
 
     lax.fori_loop(0, NCHUNK, vstart, 0)
+
+    def wcopy(d):
+        return remote(w_ref, wbuf.at[s], ws.at[d], wr.at[d], xdev(d))
+
+    def xcopies(d):
+        return [
+            remote(a, b.at[s], xs.at[n, d], xr.at[n, d], xdev(d))
+            for n, (a, b) in enumerate(((codes, codeg), (bit_ref, bitg), (dests, destg)))
+        ]
+
+    def slot(cc, zz, yy):
+        return cc * 32 + zz * 4 + yy
+
+    def zat(cc, e):
+        if EVENTS[e] is None:
+            return z
+        way, hop = EVENTS[e]
+        return lax.rem(z + 8 + (2 * cc - 1) * (1 - 2 * way) * hop, 8)
+
+    def znext(way):
+        return (s, lax.rem(z + 8 + (1 - 2 * c) * (1 - 2 * way), 8), y, c)
+
+    def event_of(way, hop):
+        return EVENTS.index((way, hop)) if hop else 0
+
+    def part_a(cc, zz, yy):
+        return tabs.at[slot(cc, zz, yy), pl.ds(0, A_ROWS), :]
+
+    def part_b(cc, zz):
+        return tabs.at[pl.ds(slot(cc, zz, 0), 4), pl.ds(A_ROWS, 256 - A_ROWS), :]
+
+    def yof(d):
+        return lax.rem(y + 4 + d, 4)
+
+    def azcopy(way, hop):
+        here = part_a(c, zat(c, event_of(way, hop - 1)), y)
+        return remote(here, here, azs.at[way, hop], azr.at[way, hop], znext(way))
+
+    def bzcopy(way, hop):
+        here = part_b(c, zat(c, event_of(way, hop - 1)))
+        return remote(here, here, bzs.at[way, hop], bzr.at[way, hop], znext(way))
+
+    def bycopy(j):
+        here = tabs.at[slot(c, z, y), pl.ds(A_ROWS, 256 - A_ROWS), :]
+        return remote(here, here, bys.at[j], byr.at[j], ydev((1, -1, 2)[j]))
+
+    def ycopy(k, e):
+        here = part_a(c, zat(c, e), y)
+        return remote(here, here, ys.at[k, e], yr.at[k, e], ydev(1 - 2 * k))
+
+    def lcopy(e):
+        sign = 1 - 2 * (e % 2)
+        here = part_a(c, zat(c, e), yof(-sign))
+        return remote(here, here, ls.at[e], lr.at[e], ydev(sign))
+
+    def ccopy(k, e, cc):
+        here = part_a(cc, zat(cc, e), yof((0, -1, 1, 2)[k]))
+        return remote(here, here, cs.at[k, e], cr.at[k, e], pair)
+
+    def cbcopy(e, cc):
+        here = part_b(cc, zat(cc, e))
+        return remote(here, here, cbs.at[e], cbr.at[e], pair)
+
+    def on_b0():
+        for j in range(3):
+            bycopy(j).wait_recv()
+        bzcopy(0, 1).start()
+        bzcopy(1, 1).start()
+        cbcopy(0, c).start()
+
+    def on_a(e):
+        way, hop = EVENTS[e]
+        azcopy(way, hop).wait_recv()
+        if hop < HOPS[way]:
+            azcopy(way, hop + 1).start()
+        ycopy(0, e).start()
+        ycopy(1, e).start()
+        ccopy(0, e, c).start()
+
+    def on_b(e):
+        way, hop = EVENTS[e]
+        bzcopy(way, hop).wait_recv()
+        if hop < HOPS[way]:
+            bzcopy(way, hop + 1).start()
+        cbcopy(e, c).start()
+
+    def on_y(e):
+        ycopy(0, e).wait_recv()
+        ycopy(1, e).wait_recv()
+        lcopy(e).start()
+        ccopy(1, e, c).start()
+        ccopy(2, e, c).start()
+
+    def on_l(e):
+        lcopy(e).wait_recv()
+        ccopy(3, e, c).start()
+
+    def pcopy(d, i):
+        at = pl.ds(pl.multiple_of(i * CHUNK, CHUNK), CHUNK)
+        return remote(
+            sendbuf.at[lax.rem(s + d, 4), :, at], rbuf.at[s, :, at], ps.at[d, i], pr.at[d, i], xdev(d)
+        )
+
+    def put_table(value):
+        tabs[slot(c, z, y)] = value
+
+    pl.semaphore_wait(barrier, 38)
+    for d in (1, 3, 2):
+        wcopy(d).start()
+    build_table(s, bk_ref, bv_ref, put_table)
+
+    for j in range(3):
+        bycopy(j).start()
+    azcopy(0, 1).start()
+    azcopy(1, 1).start()
+    for k in (0, 1):
+        ycopy(k, 0).start()
+    ccopy(0, 0, c).start()
 
     for i in range(NCHUNK):
         at = slice((i % 8) * CHUNK, (i % 8 + 1) * CHUNK)
@@ -116,109 +230,67 @@
     dests[...] = jnp.zeros_like(dests)
     dests[0:2, 0:64] = (d & 1) * 32 + (d >> 3) * 4 + ((d >> 1) & 3)
 
-    def wcopy(d):
-        return remote(w_ref, wbuf.at[s], ws.at[d], wr.at[d], xdev(d))
-
-    def xcopies(d):
-        return [
-            remote(a, b.at[s], xs.at[n, d], xr.at[n, d], xdev(d))
-            for n, (a, b) in enumerate(((codes, codeg), (bit_ref, bitg), (dests, destg)))
-        ]
-
-    def slot(cc, zz, yy):
-        return cc * 32 + zz * 4 + yy
-
-    def zfrom(e):
-        return lax.rem(z + 8 - delta(e), 8)
-
-    def zcopy(e):
-        here = tabs.at[slot(c, z, y)]
-        return remote(here, here, zs.at[e], zr.at[e], zdev(e))
-
-    def ycopy(k, e):
-        here = tabs.at[slot(c, zfrom(e), y)]
-        return remote(here, here, ys.at[k, e], yr.at[k, e], ydev(1 - 2 * k))
-
-    def lcopy(e):
-        sign = 1 - 2 * (e % 2)
-        here = tabs.at[slot(c, zfrom(e), lax.rem(y + 4 - sign, 4))]
-        return remote(here, here, ls.at[e], lr.at[e], ydev(sign))
-
-    def ccopy(k, e):
-        at = (0, -1, 1, 2)[k]
-        here = tabs.at[slot(c, zfrom(e), lax.rem(y + 4 + at, 4))]
-        return remote(here, here, cs.at[k, e], cr.at[k, e], pair)
-
-    def carrive(k, e):
-        at = (0, -1, 1, 2)[k]
-        here = tabs.at[slot(1 - c, zfrom(e), lax.rem(y + 4 + at, 4))]
-        return remote(here, here, cs.at[k, e], cr.at[k, e], pair)
-
-    def pcopy(d, i):
-        at = pl.ds(pl.multiple_of(i * CHUNK, CHUNK), CHUNK)
-        return remote(
-            sendbuf.at[lax.rem(s + d, 4), :, at], rbuf.at[s, :, at], ps.at[d, i], pr.at[d, i], xdev(d)
-        )
-
-    def put_table(value):
-        tabs[slot(c, z, y)] = value
-
-    build_table(s, bk_ref, bv_ref, put_table)
-    pl.semaphore_wait(barrier, 38)
-
-    for d in (1, 3, 2):
-        wcopy(d).start()
-    for e in range(1, 8):
-        zcopy(e).start()
-    for k in (0, 1):
-        ycopy(k, 0).start()
-    ccopy(0, 0).start()
     for d in (1, 3, 2):
         for cp in xcopies(d):
             cp.start()
     own = [
         pltpu.make_async_copy(a, b.at[s], own_sem.at[n])
-        for n, (a, b) in enumerate(((codes, codeg), (bit_ref, bitg), (dests, destg), (w_ref, wbuf)))
+        for n, (a, b) in enumerate(((codes, codeg), (bit_ref, bitg), (dests, destg)))
     ]
     for cp in own:
         cp.start()
-    for cp in own:
-        cp.wait()
-    for d in (1, 2, 3):
-        wcopy(d).wait_recv()
-    w_last = wbuf[lax.rem(s + 3, 4)].astype(F32).T.astype(BF16)
-    last[pl.ds(0, 128), :] = w_last
-    eye = lax.broadcasted_iota(jnp.int32, (128, 128), 0) == lax.broadcasted_iota(jnp.int32, (128, 128), 1)
-    last[pl.ds(128, 128), :] = eye.astype(F32).astype(BF16)
-
-    def sections(i):
+    half[0] = (0.5 * w_ref[...].astype(F32)).astype(BF16)
+
+    def first_section(i, carry):
         at = pl.ds(pl.multiple_of(i * CHUNK, CHUNK), CHUNK)
         vcopy(i).wait()
         v = vbuf[at, :]
-        for j in range(3):
-            u = jnp.dot(v, wbuf[lax.rem(s + j, 4)], preferred_element_type=F32)
-            v = silu_add(v.astype(F32), u)
+        vbuf[at, :] = silu_add(v.astype(F32), jnp.dot(v, half[0], preferred_element_type=F32))
+        return carry
+
+    lax.fori_loop(0, NCHUNK, first_section, 0)
+    on_b0()
+    on_a(1)
+    on_a(2)
+    for d in (1, 2, 3):
+        wcopy(d).wait_recv()
+    for j in (1, 2):
+        half[j] = (0.5 * wbuf[lax.rem(s + j, 4)].astype(F32)).astype(BF16)
+    last[pl.ds(0, 128), :] = (0.5 * wbuf[lax.rem(s + 3, 4)].astype(F32)).T.astype(BF16)
+    eye = lax.broadcasted_iota(jnp.int32, (128, 128), 0) == lax.broadcasted_iota(jnp.int32, (128, 128), 1)
+    last[pl.ds(128, 128), :] = eye.astype(F32).astype(BF16)
+
+    def sections(i):
+        at = pl.ds(pl.multiple_of(i * CHUNK, CHUNK), CHUNK)
+        v = vbuf[at, :]
+        for j in (1, 2):
+            v = silu_add(v.astype(F32), jnp.dot(v, half[j], preferred_element_type=F32))
         out = lax.dot_general(last[...], v, NT, preferred_element_type=F32)
         v = silu_add(out[128:], out[:128])
         for q in range(4):
             sendbuf[q, :, at] = v[q * COLS : (q + 1) * COLS]
 
     sections(0)
+    during = {
+        1: [(on_y, 0)],
+        6: [(on_l, 0)],
+        7: [(on_a, 3), (on_a, 4)],
+        8: [(on_b, 1), (on_b, 2)],
+        10: [(on_y, 1), (on_y, 2)],
+        14: [(on_a, 5), (on_a, 6)],
+        15: [(on_l, 1), (on_l, 2)],
+    }
 
     def step(i, carry):
         sections(i)
         for d in (1, 3, 2):
             pcopy(d, i - 1).start()
-
-        @pl.when(i % 2 == 1)
-        def _():
-            @pl.when(i < 14)
-            def _():
-                e = i // 2 + 1
-                zcopy(e).wait_recv()
-                for k in (0, 1):
-                    ycopy(k, e).start()
-                ccopy(0, e).start()
+        for at, todo in during.items():
+
+            @pl.when(i == at)
+            def _(todo=todo):
+                for act, e in todo:
+                    act(e)
 
         return carry
 
@@ -227,7 +299,14 @@
     own_p.start()
     for d in (1, 3, 2):
         pcopy(d, NCHUNK - 1).start()
-
+    on_b(3)
+    on_b(4)
+    on_y(3)
+    on_y(4)
+    on_a(7)
+
+    for cp in own:
+        cp.wait()
     for d in (1, 2, 3):
         for cp in xcopies(d):
             cp.wait_recv()
@@ -245,79 +324,79 @@
     to_scalar.wait()
     own_p.wait()
     acc_ref[...] = jnp.zeros_like(acc_ref)
-    hot1[...] = jnp.zeros_like(hot1)
-    wide1[...] = jnp.zeros_like(wide1)
-
-    def near(e, carry):
-        ycopy(0, e).wait_recv()
-        ycopy(1, e).wait_recv()
-        lcopy(e).start()
-        ccopy(1, e).start()
-        ccopy(2, e).start()
-        return carry
-
-    lax.fori_loop(0, 8, near, 0)
-
-    def far(e, carry):
-        lcopy(e).wait_recv()
-        ccopy(3, e).start()
-        return carry
-
-    lax.fori_loop(0, 8, far, 0)
-
-    def finish(e, carry):
+    on_l(3)
+    on_l(4)
+    on_b(5)
+    on_b(6)
+    on_y(5)
+    on_y(6)
+    on_l(5)
+    on_l(6)
+    on_b(7)
+    on_y(7)
+    on_l(7)
+    for e in range(8):
         for k in range(4):
-            carrive(k, e).wait_recv()
-        return carry
-
-    lax.fori_loop(0, 8, finish, 0)
+            ccopy(k, e, 1 - c).wait_recv()
+        cbcopy(e, 1 - c).wait_recv()
 
     one, zero = jnp.ones((), BF16), jnp.zeros((), BF16)
     rows256 = lax.broadcasted_iota(jnp.int32, (256, 128), 0).astype(F32).astype(BF16)
     rows128 = lax.broadcasted_iota(jnp.int32, (128, 128), 0).astype(F32).astype(BF16)
 
-    def gather(src, i, hot_ref, wide_ref):
+    def permuted(entry, code):
+        lane = jnp.broadcast_to(code & 127, (8, 128))
+        part = jnp.broadcast_to((code >> 7) & 15, (8, 128))
+        here = [part == p for p in range(16)]
+        got = []
+        for r in range(0, COLS, 16):
+            for p in range(16):
+                rows = slice(p // 2 * COLS + r, p // 2 * COLS + r + 16)
+                tile = tabs[entry, rows, p % 2 * 128 : p % 2 * 128 + 128].astype(F32)
+                new = [jnp.take_along_axis(tile[h : h + 8], lane, axis=1) for h in (0, 8)]
+                held = new if p == 0 else [jnp.where(here[p], n, o) for n, o in zip(new, held)]
+            got += held
+        return jnp.concatenate(got, axis=0)
+
+    def join_chunk(src, i):
         code = codeg[src, pl.ds(i, 1), :]
         kept = kept_ref[i % 8, pl.ds(2 * src + i // 8, 1), :]
         low = (code & 255).astype(F32).astype(BF16)
         high = (code >> 8) & 7
         glow = (code >> 11) & 7
         ghigh = jnp.where(kept == 1, code >> 14, -1).astype(F32).astype(BF16)
+        wide, hots = [], []
         for b in range(CHUNK // 128):
             at = slice(b * 128, (b + 1) * 128)
-            hot = jnp.where(rows256 == low[:, at], one, zero)
-            table = tabs[where_ref[src, i // 8, (i % 8) * 8 + b]]
-            out = jnp.dot(table, hot, preferred_element_type=F32)
-            matched = jnp.zeros((COLS, 128), F32)
-            for p in range(8):
-                matched = jnp.where(high[:, at] == p, out[p * COLS : (p + 1) * COLS], matched)
+            entry = where_ref[src, i // 8, (i % 8) * 8 + b]
+            if b < PERMUTED:
+                matched = permuted(entry, code[:, at])
+            else:
+                hot = jnp.where(rows256 == low[:, at], one, zero)
+                out = jnp.dot(tabs[entry], hot, preferred_element_type=F32)
+                matched = jnp.zeros((COLS, 128), F32)
+                for p in range(8):
+                    matched = jnp.where(high[:, at] == p, out[p * COLS : (p + 1) * COLS], matched)
             pay = rbuf[src, :, pl.ds(pl.multiple_of(i * CHUNK + b * 128, 128), 128)]
             joined = pay.astype(F32) * matched
-            for p in range(8):
-                wide_ref[p * COLS : (p + 1) * COLS, at] = jnp.where(glow[:, at] == p, joined, 0.0).astype(BF16)
-            hot_ref[:, at] = jnp.where(rows128 == ghigh[:, at], one, zero)
-
-    def group(hot_ref, wide_ref):
-        acc_ref[...] += lax.dot_general(hot_ref[...], wide_ref[...], NT, preferred_element_type=F32)
-
-    def join(t, carry):
-        d = t % 4
-        i = t // 4 * 2
-        src = lax.rem(s + 4 - d, 4)
-
-        @pl.when(d > 0)
-        def _():
+            wide.append(
+                jnp.concatenate(
+                    [jnp.where(glow[:, at] == p, joined, 0.0).astype(BF16) for p in range(8)], axis=0
+                )
+            )
+            hots.append(jnp.where(rows128 == ghigh[:, at], one, zero))
+        acc_ref[...] += lax.dot_general(
+            jnp.concatenate(hots, axis=1), jnp.concatenate(wide, axis=1), NT, preferred_element_type=F32
+        )
+
+    def join(i, carry):
+        for d in (1, 2, 3):
             pcopy(d, i).wait_recv()
-            pcopy(d, i + 1).wait_recv()
-
-        group(hot1, wide1)
-        gather(src, i, hot0, wide0)
-        group(hot0, wide0)
-        gather(src, i + 1, hot1, wide1)
-        return carry
-
-    lax.fori_loop(0, 32, join, 0)
-    group(hot1, wide1)
+        for d in range(4):
+            join_chunk(lax.rem(s + 4 - d, 4), i)
+        return carry
+
+    lax.fori_loop(0, NCHUNK, join, 0)
 
     def piece(px, pc):
         return (
@@ -338,21 +417,19 @@
     rows, lanes = piece(s, c)
     first[me] = acc_ref[rows, lanes]
 
-    def sent_e(e, carry):
+    for e in range(8):
         for k in range(4):
-            ccopy(k, e).wait_send()
+            ccopy(k, e, c).wait_send()
+        cbcopy(e, c).wait_send()
         for k in (0, 1):
             ycopy(k, e).wait_send()
         lcopy(e).wait_send()
-        return carry
-
-    lax.fori_loop(0, 8, sent_e, 0)
-
-    def sent_z(e, carry):
-        zcopy(e).wait_send()
-        return carry
-
-    lax.fori_loop(1, 8, sent_z, 0)
+    for way in (0, 1):
+        for hop in range(1, HOPS[way] + 1):
+            azcopy(way, hop).wait_send()
+            bzcopy(way, hop).wait_send()
+    for j in range(3):
+        bycopy(j).wait_send()
 
     def sent_p(i, carry):
         for d in (1, 2, 3):
@@ -412,6 +489,7 @@
             pltpu.VMEM((4, COLS, ROWS), BF16),
             pltpu.VMEM((64, 256, 256), BF16),
             pltpu.VMEM((4, 128, 128), BF16),
+            pltpu.VMEM((3, 128, 128), BF16),
             pltpu.VMEM((256, 128), BF16),
             pltpu.VMEM((NCHUNK, CHUNK), i32),
             pltpu.VMEM((4, NCHUNK, CHUNK), i32),
@@ -420,19 +498,15 @@
             pltpu.VMEM((4, 8, 128), i32),
             pltpu.SMEM((4, 8, 128), i32),
             pltpu.VMEM((8, 8, CHUNK), i32),
-            pltpu.VMEM((128, CHUNK), BF16),
-            pltpu.VMEM((128, CHUNK), BF16),
-            pltpu.VMEM((256, CHUNK), BF16),
-            pltpu.VMEM((256, CHUNK), BF16),
             pltpu.VMEM((128, 256), F32),
             pltpu.VMEM((8, 32, 128), F32),
             pltpu.VMEM((32, 4, 128), F32),
             pltpu.VMEM((32, 4, 128), F32),
             dma((NCHUNK,)),
             dma((4,)), dma((4,)), dma((3, 4)), dma((3, 4)),
-            dma((8,)), dma((8,)),
+            dma((2, 5)), dma((2, 5)), dma((2, 5)), dma((2, 5)), dma((3,)), dma((3,)),
             dma((2, 8)), dma((2, 8)), dma((8,)), dma((8,)),
-            dma((4, 8)), dma((4, 8)),
+            dma((4, 8)), dma((4, 8)), dma((8,)), dma((8,)),
             dma((4, NCHUNK)), dma((4, NCHUNK)),
             dma((6,)),
             dma((8,)), dma((8,)), dma((32,)), dma((32,)),

time: 106 us -> 90.8 us (0.86)
  Pallas kernels: 105 us -> 89.4 us
    pallas_call x1, Pallas kernels: 105 us -> 89.4 us  [local(): pl.pallas_call(fused_kernel, name='fused', out_shape=jax.ShapeDtypeStruct...]
where the time goes in v3:
time: 90.8 us; the launch traced here: 90.7 us
  Pallas kernels  89.4 us (98%)
  local copies, waits for them, and re-layouts  1.26 us (1%)
    pallas_call x1, Pallas kernels, local(): pl.pallas_call(fused_kernel, name='fused', out_shape=jax.ShapeDtypeStruct...  89.4 us

profile of v3, /device:TPU:1, one launch (start us, length us, event | category | flops | bytes accessed | tf_op | source)
XLA Modules:
  0.0 90.7 jit_solution(4396192654062142122)
XLA Ops:
  0.0 89.4 %fused.1 = f32[4,128]{1,0:T(4,128)} custom-call(bf16[128,128]{1,0:T(8,128)(2,1)} %bitcast.6, bf16[16384,128]{1,0:T(8,128)(2,1)} %bitcast.5, s32[2,8192]{1,0:T(2,128)} %key_ref.1, s32[2,8192]{1,0:T(2,128)} %grp_ref.1, s32[2,64]{1,0:T(2,128)} %bitcast.9, s32[8,512]{1,0:T(8,128)} %bitcast.7, s32[1,4096]{1,0:T(1,128)} %bitcast.8, bf16[4096,128]{1,0:T(8,128)(2,1)} %bv_ref.1), custom_call_target="tpu_custom_call" | custom-call | tf_op jit(solution)/shard_map/fused/pallas_call | solution.py:480
  89.4 1.3 %copy.10 = f32[4,128]{1,0:T(4,128)} copy(f32[4,128]{1,0:T(4,128)} %fused.1) | data formatting | bytes 4096

commit v4 on v3

--- a/solution.py
+++ b/solution.py
@@ -19,6 +19,7 @@
 NCHUNK = ROWS // CHUNK
 BUILD = 4096
 PERMUTED = 4
+EARLY = 6
 A_ROWS = 176
 HOPS = (4, 3)
 EVENTS = (None, (0, 1), (1, 1), (0, 2), (1, 2), (0, 3), (1, 3), (0, 4))
@@ -58,8 +59,8 @@
 
 
 def fused_kernel(
-    w_ref, v_hbm, key_ref, grp_ref, dst_ref, bit_ref, bk_ref, bv_ref, out_ref,
-    vbuf, sendbuf, rbuf, tabs, wbuf, half, last, codes, codeg, bitg, dests, destg, where_ref, kept_ref,
+    w_ref, v_hbm, key_ref, grp_ref, dst_ref, bit_ref, bk_ref, bv_hbm, out_ref,
+    vbuf, bv_ref, sendbuf, rbuf, tabs, wbuf, half, last, codes, codeg, bitg, dests, destg, where_ref, kept_ref,
     acc_ref, first, mid, second,
     vs, ws, wr, xs, xr, azs, azr, bzs, bzr, bys, byr, ys, yr, ls, lr, cs, cr, cbs, cbr, ps, pr, own_sem, s1, r1, s2, r2,
 ):
@@ -102,6 +103,8 @@
         vcopy(i).start()
         return carry
 
+    bv_copy = pltpu.make_async_copy(bv_hbm, bv_ref, own_sem.at[3])
+    bv_copy.start()
     lax.fori_loop(0, NCHUNK, vstart, 0)
 
     def wcopy(d):
@@ -212,6 +215,7 @@
     pl.semaphore_wait(barrier, 38)
     for d in (1, 3, 2):
         wcopy(d).start()
+    bv_copy.wait()
     build_table(s, bk_ref, bv_ref, put_table)
 
     for j in range(3):
@@ -248,7 +252,7 @@
         vbuf[at, :] = silu_add(v.astype(F32), jnp.dot(v, half[0], preferred_element_type=F32))
         return carry
 
-    lax.fori_loop(0, NCHUNK, first_section, 0)
+    lax.fori_loop(0, EARLY, first_section, 0)
     on_b0()
     on_a(1)
     on_a(2)
@@ -260,32 +264,42 @@
     eye = lax.broadcasted_iota(jnp.int32, (128, 128), 0) == lax.broadcasted_iota(jnp.int32, (128, 128), 1)
     last[pl.ds(128, 128), :] = eye.astype(F32).astype(BF16)
 
-    def sections(i):
+    def sections(i, todo):
         at = pl.ds(pl.multiple_of(i * CHUNK, CHUNK), CHUNK)
+        if 0 in todo:
+            vcopy(i).wait()
         v = vbuf[at, :]
-        for j in (1, 2):
+        for j in todo:
             v = silu_add(v.astype(F32), jnp.dot(v, half[j], preferred_element_type=F32))
         out = lax.dot_general(last[...], v, NT, preferred_element_type=F32)
         v = silu_add(out[128:], out[:128])
         for q in range(4):
             sendbuf[q, :, at] = v[q * COLS : (q + 1) * COLS]
 
-    sections(0)
+    sections(0, (1, 2))
     during = {
         1: [(on_y, 0)],
-        6: [(on_l, 0)],
-        7: [(on_a, 3), (on_a, 4)],
-        8: [(on_b, 1), (on_b, 2)],
-        10: [(on_y, 1), (on_y, 2)],
-        14: [(on_a, 5), (on_a, 6)],
-        15: [(on_l, 1), (on_l, 2)],
+        2: [(on_a, 3), (on_a, 4)],
+        4: [(on_y, 1), (on_y, 2)],
+        5: [(on_l, 0)],
+        6: [(on_b, 1), (on_b, 2)],
+        8: [(on_a, 5), (on_a, 6)],
+        9: [(on_l, 1), (on_l, 2)],
+        10: [(on_y, 3), (on_y, 4)],
+        11: [(on_b, 3), (on_b, 4)],
+        12: [(on_a, 7)],
+        13: [(on_l, 3), (on_l, 4)],
+        14: [(on_y, 5), (on_y, 6)],
+        15: [(on_b, 5), (on_b, 6)],
     }
 
-    def step(i, carry):
-        sections(i)
+    def step(i, carry, first, sections_left):
+        sections(i, sections_left)
         for d in (1, 3, 2):
             pcopy(d, i - 1).start()
         for at, todo in during.items():
+            if (at < EARLY) != first:
+                continue
 
             @pl.when(i == at)
             def _(todo=todo):
@@ -294,16 +308,13 @@
 
         return carry
 
-    lax.fori_loop(1, NCHUNK, step, 0)
+    lax.fori_loop(1, EARLY, functools.partial(step, first=True, sections_left=(1, 2)), 0)
+    lax.fori_loop(EARLY, NCHUNK, functools.partial(step, first=False, sections_left=(0, 1, 2)), 0)
     own_p = pltpu.make_async_copy(sendbuf.at[s], rbuf.at[s], own_sem.at[4])
     own_p.start()
     for d in (1, 3, 2):
         pcopy(d, NCHUNK - 1).start()
-    on_b(3)
-    on_b(4)
-    on_y(3)
-    on_y(4)
-    on_a(7)
+    on_y(7)
 
     for cp in own:
         cp.wait()
@@ -324,17 +335,10 @@
     to_scalar.wait()
     own_p.wait()
     acc_ref[...] = jnp.zeros_like(acc_ref)
-    on_l(3)
-    on_l(4)
-    on_b(5)
-    on_b(6)
-    on_y(5)
-    on_y(6)
     on_l(5)
     on_l(6)
+    on_l(7)
     on_b(7)
-    on_y(7)
-    on_l(7)
     for e in range(8):
         for k in range(4):
             ccopy(k, e, 1 - c).wait_recv()
@@ -453,6 +457,14 @@
 
     lax.fori_loop(1, 32, send, 0)
     second[place] = mid[place]
+    for k in range(1, 8):
+        copy1(k).wait_send()
+
+    def done(k, carry):
+        copy2(k).wait_send()
+        return carry
+
+    lax.fori_loop(1, 32, done, 0)
 
     def take(k, carry):
         copy2(k).wait_recv()
@@ -463,28 +475,22 @@
     for x in range(4):
         for k in range(4):
             out_ref[k : k + 1, x * COLS : (x + 1) * COLS] = total[x : x + 1, k * COLS : (k + 1) * COLS]
-    for k in range(1, 8):
-        copy1(k).wait_send()
-
-    def done(k, carry):
-        copy2(k).wait_send()
-        return carry
-
-    lax.fori_loop(1, 32, done, 0)
 
 
 def local(probe_values, probe_keys, group_ids, block_dest, filter_bits, section_weights, build_keys, build_values):
     dma = pltpu.SemaphoreType.DMA
     vmem = pl.BlockSpec(memory_space=pltpu.VMEM)
+    hbm = pl.BlockSpec(memory_space=pl.ANY)
     i32 = jnp.int32
     return pl.pallas_call(
         fused_kernel,
         name="fused",
         out_shape=jax.ShapeDtypeStruct((4, 128), F32),
-        in_specs=[vmem, pl.BlockSpec(memory_space=pl.ANY)] + [vmem] * 6,
+        in_specs=[vmem, hbm] + [vmem] * 5 + [hbm],
         out_specs=vmem,
         scratch_shapes=[
             pltpu.VMEM((ROWS, 128), BF16),
+            pltpu.VMEM((BUILD, 128), BF16),
             pltpu.VMEM((4, COLS, ROWS), BF16),
             pltpu.VMEM((4, COLS, ROWS), BF16),
             pltpu.VMEM((64, 256, 256), BF16),

time: 90.8 us -> 86.1 us (0.948)
  Pallas kernels: 89.4 us -> 84.7 us
    pallas_call x1, Pallas kernels: 89.4 us -> 84.7 us  [local(): pl.pallas_call(fused_kernel, name='fused', out_shape=jax.ShapeDtypeStruct...]
where the time goes in v4:
time: 86.1 us; the launch traced here: 85.9 us
  Pallas kernels  84.7 us (98%)
  local copies, waits for them, and re-layouts  1.26 us (1%)
    pallas_call x1, Pallas kernels, local(): pl.pallas_call(fused_kernel, name='fused', out_shape=jax.ShapeDtypeStruct...  84.7 us

profile of v4, /device:TPU:1, one launch (start us, length us, event | category | flops | bytes accessed | tf_op | source)
XLA Modules:
  0.0 85.9 jit_solution(7788612982788574345)
XLA Ops:
  0.0 84.7 %fused.1 = f32[4,128]{1,0:T(4,128)} custom-call(bf16[128,128]{1,0:T(8,128)(2,1)} %bitcast.6, bf16[16384,128]{1,0:T(8,128)(2,1)} %bitcast.5, s32[2,8192]{1,0:T(2,128)} %key_ref.1, s32[2,8192]{1,0:T(2,128)} %grp_ref.1, s32[2,64]{1,0:T(2,128)} %bitcast.9, s32[8,512]{1,0:T(8,128)} %bitcast.7, s32[1,4096]{1,0:T(1,128)} %bitcast.8, bf16[4096,128]{1,0:T(8,128)(2,1)} %bv_hbm.1), custom_call_target="tpu_custom_call" | custom-call | tf_op jit(solution)/shard_map/fused/pallas_call | solution.py:485
  84.7 1.3 %copy.10 = f32[4,128]{1,0:T(4,128)} copy(f32[4,128]{1,0:T(4,128)} %fused.1) | data formatting | bytes 4096
